TPU v7x, 512 devices: a whole 4x8x8 slice. The times are simulated.
512 devices in a mesh: seq: 32 (over x, z), head: 16 (over y, core).
Axes of the slice: x: 4, y: 8, z: 8, core: 2. Of those that a mesh axis runs over, the one named last changes fastest.
Arguments:
- xs: bfloat16 [49152, 5120], P('seq', 'head'), may hold values from -6 to 6
- dxs: bfloat16 [49152, 5120], P('seq', 'head'), may hold values from -6 to 6
- zgate: bfloat16 [49152, 5120], P('seq', 'head'), may hold values from -6 to 6
- bmat: bfloat16 [49152, 128], P('seq'), may hold values from -1 to 1
- cmat: bfloat16 [49152, 128], P('seq'), may hold values from -1 to 1
- dt_raw: float32 [80, 49152], P('head', 'seq'), may hold values from -3 to 3
- dt_bias: float32 [80], P('head'), may hold values from -1 to 1
- a_rate: float32 [80], P('head'), may hold values from 0 to 1, as said below
- d_skip: float32 [80], P('head'), may hold values from 0.5 to 2
- gain: float32 [5120], replicated, may hold values from 0.5 to 1.5
- traj_ids: int32 [192], P('seq'), may hold values from 0 to 9, as said below
Outputs:
- normed: bfloat16 [49152, 5120], P(('seq', 'head'))
- normed_tan: bfloat16 [49152, 5120], P(('seq', 'head'))
Inputs may be any that keep to these rules, and one draw needn't show every extreme that they name: `traj_ids`: never falling from one block to the next; trajectory 0 spans exactly the first 96 blocks, trajectory 1 the next 6 blocks or more, every other trajectory one block or more. `a_rate`: positive.
All inputs are finite; a program needn't handle non-finite values.
Results may differ from a plain program's by a relative error of at most 0.0057.
Values may be sent and summed in bfloat16 or wider, within the bound.
No kernel may reach another device: no remote copies, remote signals or barrier semaphores. Data moves between devices by JAX's collectives and lax.ppermute only.
A program may use at most 128 MiB of HBM per device.

v0:
```python
import jax
import jax.numpy as jnp
from jax import lax
from jax.sharding import PartitionSpec as P

Q = 256


def passed_along(block, axis, distance):
    devices = range(lax.axis_size(axis))
    route = [(i - distance, i) for i in devices if i - distance in devices]
    return lax.ppermute(block, axis, route)


def local_block(joined, b_block, c_block, step_block, log_block, state_in):
    token_count = joined.shape[0]
    scores = jnp.dot(c_block, b_block.T, preferred_element_type=jnp.float32)
    places = jnp.arange(token_count)
    causal_mask = places[:, None] >= places[None, :]
    log_gap = log_block[:, :, None] - log_block[:, None, :]
    decay_table = jnp.exp(jnp.where(causal_mask[None], log_gap, -jnp.inf))
    weights = (scores[None] * decay_table * step_block[:, None, :]).astype(jnp.bfloat16)
    y_diag = jnp.einsum("hts,shp->thp", weights, joined, preferred_element_type=jnp.float32)
    end_log = log_block[:, -1]
    weight_in = step_block * jnp.exp(end_log[:, None] - log_block)
    weighted = (joined * weight_in.T[:, :, None]).astype(jnp.bfloat16)
    block_state = jnp.einsum("shp,sn->hpn", weighted, b_block, preferred_element_type=jnp.float32)
    y_off = (
        jnp.einsum(
            "tn,hpn->thp", c_block.astype(jnp.float32), state_in, precision=lax.Precision.HIGHEST
        )
        * jnp.exp(log_block).T[:, :, None]
    )
    leaving = jnp.exp(end_log)[:, None, None] * state_in + block_state
    return (y_diag + y_off, leaving)


def gate_rows(y_main, y_tan, gate_in):
    gate_value = jax.nn.silu(gate_in.astype(jnp.float32))
    return (y_main.astype(jnp.float32) * gate_value, y_tan.astype(jnp.float32) * gate_value)


def norm_rows(gated, gated_tan, square_sum, cross_sum, total_width, gain_part):
    mean_square = square_sum[:, None] / total_width
    mean_cross = cross_sum[:, None] / total_width
    inv_rms = lax.rsqrt(mean_square + 1e-05)
    normed = (gain_part * gated * inv_rms).astype(jnp.bfloat16)
    normed_tan = (gain_part * (gated_tan * inv_rms - gated * inv_rms**3 * mean_cross)).astype(
        jnp.bfloat16
    )
    return (normed, normed_tan)


def local(xs, dxs, zgate, bmat, cmat, dt_raw, dt_bias, a_rate, d_skip, gain, traj_ids):
    token_rows = xs.shape[0]
    head_count = dt_raw.shape[0]
    head_width = xs.shape[1] // head_count
    state_width = bmat.shape[1]
    block_count = token_rows // Q
    step_size = jax.nn.softplus(dt_raw + dt_bias[:, None])
    step_blocks = step_size.reshape(head_count, block_count, Q).transpose(1, 0, 2)
    log_blocks = jnp.cumsum(-(step_blocks * a_rate[None, :, None]), axis=-1)
    joined = jnp.concatenate(
        [
            xs.reshape(block_count, Q, head_count, head_width),
            dxs.reshape(block_count, Q, head_count, head_width),
        ],
        axis=-1,
    )
    b_blocks = bmat.reshape(block_count, Q, state_width)
    c_blocks = cmat.reshape(block_count, Q, state_width)
    prior_id = passed_along(traj_ids[-1:] + 1, "seq", 1)
    first_keep = (prior_id[0] == traj_ids[0] + 1).astype(jnp.float32)
    keep_next = jnp.concatenate(
        [(traj_ids[1:] == traj_ids[:-1]).astype(jnp.float32), jnp.ones((1,), jnp.float32)]
    )

    def advance(carried, item):
        state_in, factor = carried
        joined_block, b_block, c_block, step_block, log_block, keep_flag = item
        y_block, leaving = local_block(
            joined_block, b_block, c_block, step_block, log_block, state_in
        )
        end_decay = jnp.exp(log_block[:, -1])
        return ((keep_flag * leaving, keep_flag * end_decay * factor), (y_block, factor))

    zero_state = jnp.zeros((head_count, 2 * head_width, state_width), jnp.float32)
    unit_factor = jnp.ones((head_count,), jnp.float32)
    items = (joined, b_blocks, c_blocks, step_blocks, log_blocks, keep_next)
    (dev_state, dev_factor), (y_local, factors) = lax.scan(
        advance, (zero_state, first_keep * unit_factor), items
    )

    def relay(turn_index, incoming_state):
        return passed_along(dev_factor[:, None, None] * incoming_state + dev_state, "seq", 1)

    incoming = lax.fori_loop(0, lax.axis_size("seq") - 1, relay, zero_state)
    carried_in = jnp.einsum(
        "ctn,hpn->cthp", c_blocks.astype(jnp.float32), incoming, precision=lax.Precision.HIGHEST
    )
    scaling = (factors[:, :, None] * jnp.exp(log_blocks)).transpose(0, 2, 1)[..., None]
    y_total = y_local + carried_in * scaling + joined * d_skip[None, None, :, None]
    y_joined = y_total.reshape(token_rows, head_count, 2 * head_width).astype(jnp.bfloat16)
    y_main = y_joined[:, :, :head_width].reshape(token_rows, head_count * head_width)
    y_tan = y_joined[:, :, head_width:].reshape(token_rows, head_count * head_width)
    local_width = head_count * head_width
    total_width = local_width * lax.axis_size("head")
    tok_main, tok_tan, tok_gate = (
        lax.all_to_all(y_main, "head", split_axis=0, concat_axis=1, tiled=True),
        lax.all_to_all(y_tan, "head", split_axis=0, concat_axis=1, tiled=True),
        lax.all_to_all(zgate, "head", split_axis=0, concat_axis=1, tiled=True),
    )
    gated, gated_tan = gate_rows(tok_main, tok_tan, tok_gate)
    normed, normed_tan = norm_rows(
        gated,
        gated_tan,
        jnp.sum(gated * gated, axis=-1),
        jnp.sum(gated * gated_tan, axis=-1),
        total_width,
        gain,
    )
    return (normed, normed_tan)


def solution(mesh):
    placed = (
        P("seq", "head"),
        P("seq", "head"),
        P("seq", "head"),
        P("seq", None),
        P("seq", None),
        P("head", "seq"),
        P("head"),
        P("head"),
        P("head"),
        P(),
        P("seq"),
    )
    return jax.shard_map(
        local,
        mesh=mesh,
        in_specs=placed,
        out_specs=(P(("seq", "head"), None), P(("seq", "head"), None)),
        check_vma=False,
    )
```

profile of v0, /device:TPU:7, one launch (start us, length us, event | category | flops | bytes accessed | tf_op | source)
XLA Modules:
  0.0 572.8 jit_solution(5450641266811072440)
XLA Ops:
  9.8 8.8 %all-to-all-start.1 = ((bf16[16,96,320]{2,1,0:T(8,128)(2,1)}), bf16[16,96,320]{2,1,0:T(8,128)(2,1)}, u32[]{:S(2)}, u32[]{:S(2)}) async-start(bf16[16,96,320]{2,1,0:T(8,128)(2,1)} %bitcast.14), calls=%async_computation.1 | async-start | bytes 2359296 | tf_op jit(solution)/shard_map/all_to_all | solution.py:111
  20.2 9.0 %reduce-window.6 = f32[6,5,2,128]{3,2,1,0:T(2,128)S(1)} reduce-window(f32[6,5,2,128]{3,2,1,0:T(2,128)S(1)} %copy.83, f32[]{:T(128)} %constant.34.clone.1), window={size=1x1x1x128 pad=0_0x0_0x0_0x127_0}, to_apply=%region_0.1 | reduce-window | flops 975360 | bytes 61444 | tf_op jit(solution)/shard_map/reduce-window
  37.7 49.3 %while.28 = (s32[]{:T(128)}, f32[5,128,128]{2,1,0:T(8,128)S(1)}, f32[5]{0:T(128)S(1)}, f32[6,256,5,128]{1,3,0,2:T(8,128)}, f32[6,5]{1,0:T(8,128)S(1)}, /*index=5...) while((s32[]{:T(128)}, f32[5,128,128]{2,1,0:T(8,128)S(1)}, ...), condition=%wide.region_3.4_spmd.clone, body=%wide.region_2.3_spmd.clone.sunk | while | flops 397199872 | bytes 4651875 | solution.py:90
  87.3 350.4 %while.27 = (s32[]{:T(128)}, f32[5,128,128]{2,1,0:T(8,128)S(1)}, f32[5]{0:T(128)S(1)}, f32[5,128,128]{2,1,0:T(8,128)S(1)}, s32[]{:T(128)}) while((s32[]{:T(128)}, f32[5,128,128]{2,1,0:T(8,128)S(1)}, f32[5]{0:T(128)S(1)}, f32[5,128,128]{2,1,0:T(8,128)S(1)}, s32[]{:T(128)}) %tuple.59), condition=%wide.region_5.6_spmd, body=%wide.region_4.5_spmd.sunk | while | flops 163842 | bytes 2293881 | solution.py:97
  91.4 12.5 %collective-permute-done = f32[5,128,128]{2,1,0:T(8,128)S(1)} collective-permute-done((f32[5,128,128]{2,1,0:T(8,128)S(1)}, f32[5,128,128]{2,1,0:T(8,128)S(1)}, u32[]{:S(2)}, u32[]{:S(2)}) %collective-permute-start) | collective-permute-done | bytes 327712 | tf_op jit(solution)/shard_map/while/body/eval_jaxpr/ppermute | solution.py:12
  105.9 10.6 %collective-permute-done = f32[5,128,128]{2,1,0:T(8,128)S(1)} collective-permute-done((f32[5,128,128]{2,1,0:T(8,128)S(1)}, f32[5,128,128]{2,1,0:T(8,128)S(1)}, u32[]{:S(2)}, u32[]{:S(2)}) %collective-permute-start) | collective-permute-done | bytes 327712 | tf_op jit(solution)/shard_map/while/body/eval_jaxpr/ppermute | solution.py:12
  118.5 9.7 %collective-permute-done = f32[5,128,128]{2,1,0:T(8,128)S(1)} collective-permute-done((f32[5,128,128]{2,1,0:T(8,128)S(1)}, f32[5,128,128]{2,1,0:T(8,128)S(1)}, u32[]{:S(2)}, u32[]{:S(2)}) %collective-permute-start) | collective-permute-done | bytes 327712 | tf_op jit(solution)/shard_map/while/body/eval_jaxpr/ppermute | solution.py:12
  130.2 8.7 %collective-permute-done = f32[5,128,128]{2,1,0:T(8,128)S(1)} collective-permute-done((f32[5,128,128]{2,1,0:T(8,128)S(1)}, f32[5,128,128]{2,1,0:T(8,128)S(1)}, u32[]{:S(2)}, u32[]{:S(2)}) %collective-permute-start) | collective-permute-done | bytes 327712 | tf_op jit(solution)/shard_map/while/body/eval_jaxpr/ppermute | solution.py:12
  141.0 8.0 %collective-permute-done = f32[5,128,128]{2,1,0:T(8,128)S(1)} collective-permute-done((f32[5,128,128]{2,1,0:T(8,128)S(1)}, f32[5,128,128]{2,1,0:T(8,128)S(1)}, u32[]{:S(2)}, u32[]{:S(2)}) %collective-permute-start) | collective-permute-done | bytes 327712 | tf_op jit(solution)/shard_map/while/body/eval_jaxpr/ppermute | solution.py:12
  151.0 8.0 %collective-permute-done = f32[5,128,128]{2,1,0:T(8,128)S(1)} collective-permute-done((f32[5,128,128]{2,1,0:T(8,128)S(1)}, f32[5,128,128]{2,1,0:T(8,128)S(1)}, u32[]{:S(2)}, u32[]{:S(2)}) %collective-permute-start) | collective-permute-done | bytes 327712 | tf_op jit(solution)/shard_map/while/body/eval_jaxpr/ppermute | solution.py:12
  161.1 8.0 %collective-permute-done = f32[5,128,128]{2,1,0:T(8,128)S(1)} collective-permute-done((f32[5,128,128]{2,1,0:T(8,128)S(1)}, f32[5,128,128]{2,1,0:T(8,128)S(1)}, u32[]{:S(2)}, u32[]{:S(2)}) %collective-permute-start) | collective-permute-done | bytes 327712 | tf_op jit(solution)/shard_map/while/body/eval_jaxpr/ppermute | solution.py:12
  171.1 8.0 %collective-permute-done = f32[5,128,128]{2,1,0:T(8,128)S(1)} collective-permute-done((f32[5,128,128]{2,1,0:T(8,128)S(1)}, f32[5,128,128]{2,1,0:T(8,128)S(1)}, u32[]{:S(2)}, u32[]{:S(2)}) %collective-permute-start) | collective-permute-done | bytes 327712 | tf_op jit(solution)/shard_map/while/body/eval_jaxpr/ppermute | solution.py:12
  181.1 8.8 %collective-permute-done = f32[5,128,128]{2,1,0:T(8,128)S(1)} collective-permute-done((f32[5,128,128]{2,1,0:T(8,128)S(1)}, f32[5,128,128]{2,1,0:T(8,128)S(1)}, u32[]{:S(2)}, u32[]{:S(2)}) %collective-permute-start) | collective-permute-done | bytes 327712 | tf_op jit(solution)/shard_map/while/body/eval_jaxpr/ppermute | solution.py:12
  192.0 9.9 %collective-permute-done = f32[5,128,128]{2,1,0:T(8,128)S(1)} collective-permute-done((f32[5,128,128]{2,1,0:T(8,128)S(1)}, f32[5,128,128]{2,1,0:T(8,128)S(1)}, u32[]{:S(2)}, u32[]{:S(2)}) %collective-permute-start) | collective-permute-done | bytes 327712 | tf_op jit(solution)/shard_map/while/body/eval_jaxpr/ppermute | solution.py:12
  204.0 11.0 %collective-permute-done = f32[5,128,128]{2,1,0:T(8,128)S(1)} collective-permute-done((f32[5,128,128]{2,1,0:T(8,128)S(1)}, f32[5,128,128]{2,1,0:T(8,128)S(1)}, u32[]{:S(2)}, u32[]{:S(2)}) %collective-permute-start) | collective-permute-done | bytes 327712 | tf_op jit(solution)/shard_map/while/body/eval_jaxpr/ppermute | solution.py:12
  217.0 11.1 %collective-permute-done = f32[5,128,128]{2,1,0:T(8,128)S(1)} collective-permute-done((f32[5,128,128]{2,1,0:T(8,128)S(1)}, f32[5,128,128]{2,1,0:T(8,128)S(1)}, u32[]{:S(2)}, u32[]{:S(2)}) %collective-permute-start) | collective-permute-done | bytes 327712 | tf_op jit(solution)/shard_map/while/body/eval_jaxpr/ppermute | solution.py:12
  230.2 10.2 %collective-permute-done = f32[5,128,128]{2,1,0:T(8,128)S(1)} collective-permute-done((f32[5,128,128]{2,1,0:T(8,128)S(1)}, f32[5,128,128]{2,1,0:T(8,128)S(1)}, u32[]{:S(2)}, u32[]{:S(2)}) %collective-permute-start) | collective-permute-done | bytes 327712 | tf_op jit(solution)/shard_map/while/body/eval_jaxpr/ppermute | solution.py:12
  242.4 9.3 %collective-permute-done = f32[5,128,128]{2,1,0:T(8,128)S(1)} collective-permute-done((f32[5,128,128]{2,1,0:T(8,128)S(1)}, f32[5,128,128]{2,1,0:T(8,128)S(1)}, u32[]{:S(2)}, u32[]{:S(2)}) %collective-permute-start) | collective-permute-done | bytes 327712 | tf_op jit(solution)/shard_map/while/body/eval_jaxpr/ppermute | solution.py:12
  253.7 8.4 %collective-permute-done = f32[5,128,128]{2,1,0:T(8,128)S(1)} collective-permute-done((f32[5,128,128]{2,1,0:T(8,128)S(1)}, f32[5,128,128]{2,1,0:T(8,128)S(1)}, u32[]{:S(2)}, u32[]{:S(2)}) %collective-permute-start) | collective-permute-done | bytes 327712 | tf_op jit(solution)/shard_map/while/body/eval_jaxpr/ppermute | solution.py:12
  264.1 8.0 %collective-permute-done = f32[5,128,128]{2,1,0:T(8,128)S(1)} collective-permute-done((f32[5,128,128]{2,1,0:T(8,128)S(1)}, f32[5,128,128]{2,1,0:T(8,128)S(1)}, u32[]{:S(2)}, u32[]{:S(2)}) %collective-permute-start) | collective-permute-done | bytes 327712 | tf_op jit(solution)/shard_map/while/body/eval_jaxpr/ppermute | solution.py:12
  294.2 8.1 %collective-permute-done = f32[5,128,128]{2,1,0:T(8,128)S(1)} collective-permute-done((f32[5,128,128]{2,1,0:T(8,128)S(1)}, f32[5,128,128]{2,1,0:T(8,128)S(1)}, u32[]{:S(2)}, u32[]{:S(2)}) %collective-permute-start) | collective-permute-done | bytes 327712 | tf_op jit(solution)/shard_map/while/body/eval_jaxpr/ppermute | solution.py:12
  304.3 9.1 %collective-permute-done = f32[5,128,128]{2,1,0:T(8,128)S(1)} collective-permute-done((f32[5,128,128]{2,1,0:T(8,128)S(1)}, f32[5,128,128]{2,1,0:T(8,128)S(1)}, u32[]{:S(2)}, u32[]{:S(2)}) %collective-permute-start) | collective-permute-done | bytes 327712 | tf_op jit(solution)/shard_map/while/body/eval_jaxpr/ppermute | solution.py:12
  315.5 10.2 %collective-permute-done = f32[5,128,128]{2,1,0:T(8,128)S(1)} collective-permute-done((f32[5,128,128]{2,1,0:T(8,128)S(1)}, f32[5,128,128]{2,1,0:T(8,128)S(1)}, u32[]{:S(2)}, u32[]{:S(2)}) %collective-permute-start) | collective-permute-done | bytes 327712 | tf_op jit(solution)/shard_map/while/body/eval_jaxpr/ppermute | solution.py:12
  327.8 11.5 %collective-permute-done = f32[5,128,128]{2,1,0:T(8,128)S(1)} collective-permute-done((f32[5,128,128]{2,1,0:T(8,128)S(1)}, f32[5,128,128]{2,1,0:T(8,128)S(1)}, u32[]{:S(2)}, u32[]{:S(2)}) %collective-permute-start) | collective-permute-done | bytes 327712 | tf_op jit(solution)/shard_map/while/body/eval_jaxpr/ppermute | solution.py:12
  341.2 11.0 %collective-permute-done = f32[5,128,128]{2,1,0:T(8,128)S(1)} collective-permute-done((f32[5,128,128]{2,1,0:T(8,128)S(1)}, f32[5,128,128]{2,1,0:T(8,128)S(1)}, u32[]{:S(2)}, u32[]{:S(2)}) %collective-permute-start) | collective-permute-done | bytes 327712 | tf_op jit(solution)/shard_map/while/body/eval_jaxpr/ppermute | solution.py:12
  354.2 10.0 %collective-permute-done = f32[5,128,128]{2,1,0:T(8,128)S(1)} collective-permute-done((f32[5,128,128]{2,1,0:T(8,128)S(1)}, f32[5,128,128]{2,1,0:T(8,128)S(1)}, u32[]{:S(2)}, u32[]{:S(2)}) %collective-permute-start) | collective-permute-done | bytes 327712 | tf_op jit(solution)/shard_map/while/body/eval_jaxpr/ppermute | solution.py:12
  366.3 9.1 %collective-permute-done = f32[5,128,128]{2,1,0:T(8,128)S(1)} collective-permute-done((f32[5,128,128]{2,1,0:T(8,128)S(1)}, f32[5,128,128]{2,1,0:T(8,128)S(1)}, u32[]{:S(2)}, u32[]{:S(2)}) %collective-permute-start) | collective-permute-done | bytes 327712 | tf_op jit(solution)/shard_map/while/body/eval_jaxpr/ppermute | solution.py:12
  417.6 8.5 %collective-permute-done = f32[5,128,128]{2,1,0:T(8,128)S(1)} collective-permute-done((f32[5,128,128]{2,1,0:T(8,128)S(1)}, f32[5,128,128]{2,1,0:T(8,128)S(1)}, u32[]{:S(2)}, u32[]{:S(2)}) %collective-permute-start) | collective-permute-done | bytes 327712 | tf_op jit(solution)/shard_map/while/body/eval_jaxpr/ppermute | solution.py:12
  428.1 9.5 %collective-permute-done = f32[5,128,128]{2,1,0:T(8,128)S(1)} collective-permute-done((f32[5,128,128]{2,1,0:T(8,128)S(1)}, f32[5,128,128]{2,1,0:T(8,128)S(1)}, u32[]{:S(2)}, u32[]{:S(2)}) %collective-permute-start) | collective-permute-done | bytes 327712 | tf_op jit(solution)/shard_map/while/body/eval_jaxpr/ppermute | solution.py:12
  455.3 39.4 %all-to-all-start.2 = ((bf16[16,96,320]{2,1,0:T(8,128)(2,1)}), bf16[16,96,320]{2,1,0:T(8,128)(2,1)S(1)}, u32[]{:S(2)}, u32[]{:S(2)}) async-start(bf16[16,96,320]{2,1,0:T(8,128)(2,1)} %copy.100), calls=%async_computation.2 | async-start | bytes 2359296 | tf_op jit(solution)/shard_map/all_to_all | solution.py:110
  500.7 24.6 %all-to-all-done.2 = bf16[16,96,320]{2,1,0:T(8,128)(2,1)S(1)} async-done(((bf16[16,96,320]{2,1,0:T(8,128)(2,1)}), bf16[16,96,320]{2,1,0:T(8,128)(2,1)S(1)}, u32[]{:S(2)}, u32[]{:S(2)}) %all-to-all-start.2) | async-done | bytes 983072 | tf_op jit(solution)/shard_map/all_to_all | solution.py:110
  542.4 17.2 %all-to-all-done = bf16[16,96,320]{2,1,0:T(8,128)(2,1)S(1)} async-done(((bf16[16,96,320]{2,1,0:T(8,128)(2,1)}), bf16[16,96,320]{2,1,0:T(8,128)(2,1)S(1)}, u32[]{:S(2)}, u32[]{:S(2)}) %all-to-all-start) | async-done | bytes 983072 | tf_op jit(solution)/shard_map/all_to_all | solution.py:109
  (240 shorter events, 232.6 us)
Async XLA Ops:
  2.6 34.4 %collective-permute-start.1 = (s32[1]{0:T(128)}, s32[1]{0:T(128)}, u32[]{:S(2)}, u32[]{:S(2)}) collective-permute-start(s32[1]{0:T(128)} %add.62), channel_id=1, source_target_pairs={{0,16},{16,32},{32,48},{48,64},{64,80},{80,96},{96,112},{112,128},... | collective-permute-start | bytes 20 | tf_op jit(solution)/shard_map/ppermute | solution.py:12
  9.8 445.5 %all-to-all-start.1 = ((bf16[16,96,320]{2,1,0:T(8,128)(2,1)}), bf16[16,96,320]{2,1,0:T(8,128)(2,1)}, u32[]{:S(2)}, u32[]{:S(2)}) async-start(bf16[16,96,320]{2,1,0:T(8,128)(2,1)} %bitcast.14), calls=%async_computation.1 | async-start | bytes 2359296 | tf_op jit(solution)/shard_map/all_to_all | solution.py:111
  87.4 16.5 %collective-permute-start = (f32[5,128,128]{2,1,0:T(8,128)S(1)}, f32[5,128,128]{2,1,0:T(8,128)S(1)}, u32[]{:S(2)}, u32[]{:S(2)}) collective-permute-start(f32[5,128,128]{2,1,0:T(8,128)S(1)} %multiply_add_fusion.2), channel_id=1, source_target_pairs={{0,16},{16,32},{32,48},{48,64},{64,80},{80,96},{96,112},{112,128},... | collective-permute-start | bytes 983048 | tf_op jit(solution)/shard_map/while/body/eval_jaxpr/ppermute | solution.py:12
  104.0 12.5 %collective-permute-start = (f32[5,128,128]{2,1,0:T(8,128)S(1)}, f32[5,128,128]{2,1,0:T(8,128)S(1)}, u32[]{:S(2)}, u32[]{:S(2)}) collective-permute-start(f32[5,128,128]{2,1,0:T(8,128)S(1)} %multiply_add_fusion.2), channel_id=1, source_target_pairs={{0,16},{16,32},{32,48},{48,64},{64,80},{80,96},{96,112},{112,128},... | collective-permute-start | bytes 983048 | tf_op jit(solution)/shard_map/while/body/eval_jaxpr/ppermute | solution.py:12
  116.6 11.6 %collective-permute-start = (f32[5,128,128]{2,1,0:T(8,128)S(1)}, f32[5,128,128]{2,1,0:T(8,128)S(1)}, u32[]{:S(2)}, u32[]{:S(2)}) collective-permute-start(f32[5,128,128]{2,1,0:T(8,128)S(1)} %multiply_add_fusion.2), channel_id=1, source_target_pairs={{0,16},{16,32},{32,48},{48,64},{64,80},{80,96},{96,112},{112,128},... | collective-permute-start | bytes 983048 | tf_op jit(solution)/shard_map/while/body/eval_jaxpr/ppermute | solution.py:12
  128.3 10.7 %collective-permute-start = (f32[5,128,128]{2,1,0:T(8,128)S(1)}, f32[5,128,128]{2,1,0:T(8,128)S(1)}, u32[]{:S(2)}, u32[]{:S(2)}) collective-permute-start(f32[5,128,128]{2,1,0:T(8,128)S(1)} %multiply_add_fusion.2), channel_id=1, source_target_pairs={{0,16},{16,32},{32,48},{48,64},{64,80},{80,96},{96,112},{112,128},... | collective-permute-start | bytes 983048 | tf_op jit(solution)/shard_map/while/body/eval_jaxpr/ppermute | solution.py:12
  139.1 9.9 %collective-permute-start = (f32[5,128,128]{2,1,0:T(8,128)S(1)}, f32[5,128,128]{2,1,0:T(8,128)S(1)}, u32[]{:S(2)}, u32[]{:S(2)}) collective-permute-start(f32[5,128,128]{2,1,0:T(8,128)S(1)} %multiply_add_fusion.2), channel_id=1, source_target_pairs={{0,16},{16,32},{32,48},{48,64},{64,80},{80,96},{96,112},{112,128},... | collective-permute-start | bytes 983048 | tf_op jit(solution)/shard_map/while/body/eval_jaxpr/ppermute | solution.py:12
  149.1 9.9 %collective-permute-start = (f32[5,128,128]{2,1,0:T(8,128)S(1)}, f32[5,128,128]{2,1,0:T(8,128)S(1)}, u32[]{:S(2)}, u32[]{:S(2)}) collective-permute-start(f32[5,128,128]{2,1,0:T(8,128)S(1)} %multiply_add_fusion.2), channel_id=1, source_target_pairs={{0,16},{16,32},{32,48},{48,64},{64,80},{80,96},{96,112},{112,128},... | collective-permute-start | bytes 983048 | tf_op jit(solution)/shard_map/while/body/eval_jaxpr/ppermute | solution.py:12
  159.1 9.9 %collective-permute-start = (f32[5,128,128]{2,1,0:T(8,128)S(1)}, f32[5,128,128]{2,1,0:T(8,128)S(1)}, u32[]{:S(2)}, u32[]{:S(2)}) collective-permute-start(f32[5,128,128]{2,1,0:T(8,128)S(1)} %multiply_add_fusion.2), channel_id=1, source_target_pairs={{0,16},{16,32},{32,48},{48,64},{64,80},{80,96},{96,112},{112,128},... | collective-permute-start | bytes 983048 | tf_op jit(solution)/shard_map/while/body/eval_jaxpr/ppermute | solution.py:12
  169.2 9.9 %collective-permute-start = (f32[5,128,128]{2,1,0:T(8,128)S(1)}, f32[5,128,128]{2,1,0:T(8,128)S(1)}, u32[]{:S(2)}, u32[]{:S(2)}) collective-permute-start(f32[5,128,128]{2,1,0:T(8,128)S(1)} %multiply_add_fusion.2), channel_id=1, source_target_pairs={{0,16},{16,32},{32,48},{48,64},{64,80},{80,96},{96,112},{112,128},... | collective-permute-start | bytes 983048 | tf_op jit(solution)/shard_map/while/body/eval_jaxpr/ppermute | solution.py:12
  179.2 10.8 %collective-permute-start = (f32[5,128,128]{2,1,0:T(8,128)S(1)}, f32[5,128,128]{2,1,0:T(8,128)S(1)}, u32[]{:S(2)}, u32[]{:S(2)}) collective-permute-start(f32[5,128,128]{2,1,0:T(8,128)S(1)} %multiply_add_fusion.2), channel_id=1, source_target_pairs={{0,16},{16,32},{32,48},{48,64},{64,80},{80,96},{96,112},{112,128},... | collective-permute-start | bytes 983048 | tf_op jit(solution)/shard_map/while/body/eval_jaxpr/ppermute | solution.py:12
  190.1 11.9 %collective-permute-start = (f32[5,128,128]{2,1,0:T(8,128)S(1)}, f32[5,128,128]{2,1,0:T(8,128)S(1)}, u32[]{:S(2)}, u32[]{:S(2)}) collective-permute-start(f32[5,128,128]{2,1,0:T(8,128)S(1)} %multiply_add_fusion.2), channel_id=1, source_target_pairs={{0,16},{16,32},{32,48},{48,64},{64,80},{80,96},{96,112},{112,128},... | collective-permute-start | bytes 983048 | tf_op jit(solution)/shard_map/while/body/eval_jaxpr/ppermute | solution.py:12
  202.0 12.9 %collective-permute-start = (f32[5,128,128]{2,1,0:T(8,128)S(1)}, f32[5,128,128]{2,1,0:T(8,128)S(1)}, u32[]{:S(2)}, u32[]{:S(2)}) collective-permute-start(f32[5,128,128]{2,1,0:T(8,128)S(1)} %multiply_add_fusion.2), channel_id=1, source_target_pairs={{0,16},{16,32},{32,48},{48,64},{64,80},{80,96},{96,112},{112,128},... | collective-permute-start | bytes 983048 | tf_op jit(solution)/shard_map/while/body/eval_jaxpr/ppermute | solution.py:12
  215.1 13.1 %collective-permute-start = (f32[5,128,128]{2,1,0:T(8,128)S(1)}, f32[5,128,128]{2,1,0:T(8,128)S(1)}, u32[]{:S(2)}, u32[]{:S(2)}) collective-permute-start(f32[5,128,128]{2,1,0:T(8,128)S(1)} %multiply_add_fusion.2), channel_id=1, source_target_pairs={{0,16},{16,32},{32,48},{48,64},{64,80},{80,96},{96,112},{112,128},... | collective-permute-start | bytes 983048 | tf_op jit(solution)/shard_map/while/body/eval_jaxpr/ppermute | solution.py:12
  228.2 12.1 %collective-permute-start = (f32[5,128,128]{2,1,0:T(8,128)S(1)}, f32[5,128,128]{2,1,0:T(8,128)S(1)}, u32[]{:S(2)}, u32[]{:S(2)}) collective-permute-start(f32[5,128,128]{2,1,0:T(8,128)S(1)} %multiply_add_fusion.2), channel_id=1, source_target_pairs={{0,16},{16,32},{32,48},{48,64},{64,80},{80,96},{96,112},{112,128},... | collective-permute-start | bytes 983048 | tf_op jit(solution)/shard_map/while/body/eval_jaxpr/ppermute | solution.py:12
  240.5 11.2 %collective-permute-start = (f32[5,128,128]{2,1,0:T(8,128)S(1)}, f32[5,128,128]{2,1,0:T(8,128)S(1)}, u32[]{:S(2)}, u32[]{:S(2)}) collective-permute-start(f32[5,128,128]{2,1,0:T(8,128)S(1)} %multiply_add_fusion.2), channel_id=1, source_target_pairs={{0,16},{16,32},{32,48},{48,64},{64,80},{80,96},{96,112},{112,128},... | collective-permute-start | bytes 983048 | tf_op jit(solution)/shard_map/while/body/eval_jaxpr/ppermute | solution.py:12
  251.8 10.3 %collective-permute-start = (f32[5,128,128]{2,1,0:T(8,128)S(1)}, f32[5,128,128]{2,1,0:T(8,128)S(1)}, u32[]{:S(2)}, u32[]{:S(2)}) collective-permute-start(f32[5,128,128]{2,1,0:T(8,128)S(1)} %multiply_add_fusion.2), channel_id=1, source_target_pairs={{0,16},{16,32},{32,48},{48,64},{64,80},{80,96},{96,112},{112,128},... | collective-permute-start | bytes 983048 | tf_op jit(solution)/shard_map/while/body/eval_jaxpr/ppermute | solution.py:12
  262.2 9.9 %collective-permute-start = (f32[5,128,128]{2,1,0:T(8,128)S(1)}, f32[5,128,128]{2,1,0:T(8,128)S(1)}, u32[]{:S(2)}, u32[]{:S(2)}) collective-permute-start(f32[5,128,128]{2,1,0:T(8,128)S(1)} %multiply_add_fusion.2), channel_id=1, source_target_pairs={{0,16},{16,32},{32,48},{48,64},{64,80},{80,96},{96,112},{112,128},... | collective-permute-start | bytes 983048 | tf_op jit(solution)/shard_map/while/body/eval_jaxpr/ppermute | solution.py:12
  272.2 9.9 %collective-permute-start = (f32[5,128,128]{2,1,0:T(8,128)S(1)}, f32[5,128,128]{2,1,0:T(8,128)S(1)}, u32[]{:S(2)}, u32[]{:S(2)}) collective-permute-start(f32[5,128,128]{2,1,0:T(8,128)S(1)} %multiply_add_fusion.2), channel_id=1, source_target_pairs={{0,16},{16,32},{32,48},{48,64},{64,80},{80,96},{96,112},{112,128},... | collective-permute-start | bytes 983048 | tf_op jit(solution)/shard_map/while/body/eval_jaxpr/ppermute | solution.py:12
  282.3 9.9 %collective-permute-start = (f32[5,128,128]{2,1,0:T(8,128)S(1)}, f32[5,128,128]{2,1,0:T(8,128)S(1)}, u32[]{:S(2)}, u32[]{:S(2)}) collective-permute-start(f32[5,128,128]{2,1,0:T(8,128)S(1)} %multiply_add_fusion.2), channel_id=1, source_target_pairs={{0,16},{16,32},{32,48},{48,64},{64,80},{80,96},{96,112},{112,128},... | collective-permute-start | bytes 983048 | tf_op jit(solution)/shard_map/while/body/eval_jaxpr/ppermute | solution.py:12
  292.3 10.0 %collective-permute-start = (f32[5,128,128]{2,1,0:T(8,128)S(1)}, f32[5,128,128]{2,1,0:T(8,128)S(1)}, u32[]{:S(2)}, u32[]{:S(2)}) collective-permute-start(f32[5,128,128]{2,1,0:T(8,128)S(1)} %multiply_add_fusion.2), channel_id=1, source_target_pairs={{0,16},{16,32},{32,48},{48,64},{64,80},{80,96},{96,112},{112,128},... | collective-permute-start | bytes 983048 | tf_op jit(solution)/shard_map/while/body/eval_jaxpr/ppermute | solution.py:12
  302.4 11.1 %collective-permute-start = (f32[5,128,128]{2,1,0:T(8,128)S(1)}, f32[5,128,128]{2,1,0:T(8,128)S(1)}, u32[]{:S(2)}, u32[]{:S(2)}) collective-permute-start(f32[5,128,128]{2,1,0:T(8,128)S(1)} %multiply_add_fusion.2), channel_id=1, source_target_pairs={{0,16},{16,32},{32,48},{48,64},{64,80},{80,96},{96,112},{112,128},... | collective-permute-start | bytes 983048 | tf_op jit(solution)/shard_map/while/body/eval_jaxpr/ppermute | solution.py:12
  313.6 12.2 %collective-permute-start = (f32[5,128,128]{2,1,0:T(8,128)S(1)}, f32[5,128,128]{2,1,0:T(8,128)S(1)}, u32[]{:S(2)}, u32[]{:S(2)}) collective-permute-start(f32[5,128,128]{2,1,0:T(8,128)S(1)} %multiply_add_fusion.2), channel_id=1, source_target_pairs={{0,16},{16,32},{32,48},{48,64},{64,80},{80,96},{96,112},{112,128},... | collective-permute-start | bytes 983048 | tf_op jit(solution)/shard_map/while/body/eval_jaxpr/ppermute | solution.py:12
  325.8 13.4 %collective-permute-start = (f32[5,128,128]{2,1,0:T(8,128)S(1)}, f32[5,128,128]{2,1,0:T(8,128)S(1)}, u32[]{:S(2)}, u32[]{:S(2)}) collective-permute-start(f32[5,128,128]{2,1,0:T(8,128)S(1)} %multiply_add_fusion.2), channel_id=1, source_target_pairs={{0,16},{16,32},{32,48},{48,64},{64,80},{80,96},{96,112},{112,128},... | collective-permute-start | bytes 983048 | tf_op jit(solution)/shard_map/while/body/eval_jaxpr/ppermute | solution.py:12
  339.3 12.9 %collective-permute-start = (f32[5,128,128]{2,1,0:T(8,128)S(1)}, f32[5,128,128]{2,1,0:T(8,128)S(1)}, u32[]{:S(2)}, u32[]{:S(2)}) collective-permute-start(f32[5,128,128]{2,1,0:T(8,128)S(1)} %multiply_add_fusion.2), channel_id=1, source_target_pairs={{0,16},{16,32},{32,48},{48,64},{64,80},{80,96},{96,112},{112,128},... | collective-permute-start | bytes 983048 | tf_op jit(solution)/shard_map/while/body/eval_jaxpr/ppermute | solution.py:12
  352.3 12.0 %collective-permute-start = (f32[5,128,128]{2,1,0:T(8,128)S(1)}, f32[5,128,128]{2,1,0:T(8,128)S(1)}, u32[]{:S(2)}, u32[]{:S(2)}) collective-permute-start(f32[5,128,128]{2,1,0:T(8,128)S(1)} %multiply_add_fusion.2), channel_id=1, source_target_pairs={{0,16},{16,32},{32,48},{48,64},{64,80},{80,96},{96,112},{112,128},... | collective-permute-start | bytes 983048 | tf_op jit(solution)/shard_map/while/body/eval_jaxpr/ppermute | solution.py:12
  364.4 11.1 %collective-permute-start = (f32[5,128,128]{2,1,0:T(8,128)S(1)}, f32[5,128,128]{2,1,0:T(8,128)S(1)}, u32[]{:S(2)}, u32[]{:S(2)}) collective-permute-start(f32[5,128,128]{2,1,0:T(8,128)S(1)} %multiply_add_fusion.2), channel_id=1, source_target_pairs={{0,16},{16,32},{32,48},{48,64},{64,80},{80,96},{96,112},{112,128},... | collective-permute-start | bytes 983048 | tf_op jit(solution)/shard_map/while/body/eval_jaxpr/ppermute | solution.py:12
  375.6 9.9 %collective-permute-start = (f32[5,128,128]{2,1,0:T(8,128)S(1)}, f32[5,128,128]{2,1,0:T(8,128)S(1)}, u32[]{:S(2)}, u32[]{:S(2)}) collective-permute-start(f32[5,128,128]{2,1,0:T(8,128)S(1)} %multiply_add_fusion.2), channel_id=1, source_target_pairs={{0,16},{16,32},{32,48},{48,64},{64,80},{80,96},{96,112},{112,128},... | collective-permute-start | bytes 983048 | tf_op jit(solution)/shard_map/while/body/eval_jaxpr/ppermute | solution.py:12
  415.7 10.4 %collective-permute-start = (f32[5,128,128]{2,1,0:T(8,128)S(1)}, f32[5,128,128]{2,1,0:T(8,128)S(1)}, u32[]{:S(2)}, u32[]{:S(2)}) collective-permute-start(f32[5,128,128]{2,1,0:T(8,128)S(1)} %multiply_add_fusion.2), channel_id=1, source_target_pairs={{0,16},{16,32},{32,48},{48,64},{64,80},{80,96},{96,112},{112,128},... | collective-permute-start | bytes 983048 | tf_op jit(solution)/shard_map/while/body/eval_jaxpr/ppermute | solution.py:12
  426.2 11.5 %collective-permute-start = (f32[5,128,128]{2,1,0:T(8,128)S(1)}, f32[5,128,128]{2,1,0:T(8,128)S(1)}, u32[]{:S(2)}, u32[]{:S(2)}) collective-permute-start(f32[5,128,128]{2,1,0:T(8,128)S(1)} %multiply_add_fusion.2), channel_id=1, source_target_pairs={{0,16},{16,32},{32,48},{48,64},{64,80},{80,96},{96,112},{112,128},... | collective-permute-start | bytes 983048 | tf_op jit(solution)/shard_map/while/body/eval_jaxpr/ppermute | solution.py:12
  455.3 70.0 %all-to-all-start.2 = ((bf16[16,96,320]{2,1,0:T(8,128)(2,1)}), bf16[16,96,320]{2,1,0:T(8,128)(2,1)S(1)}, u32[]{:S(2)}, u32[]{:S(2)}) async-start(bf16[16,96,320]{2,1,0:T(8,128)(2,1)} %copy.100), calls=%async_computation.2 | async-start | bytes 2359296 | tf_op jit(solution)/shard_map/all_to_all | solution.py:110
  525.3 34.3 %all-to-all-start = ((bf16[16,96,320]{2,1,0:T(8,128)(2,1)}), bf16[16,96,320]{2,1,0:T(8,128)(2,1)S(1)}, u32[]{:S(2)}, u32[]{:S(2)}) async-start(bf16[16,96,320]{2,1,0:T(8,128)(2,1)} %copy.95), calls=%async_computation | async-start | bytes 2359296 | tf_op jit(solution)/shard_map/all_to_all | solution.py:109
  (15 other events, 860.8 us)
where the time goes:
time: 576 us; the launch traced here: 573 us
  waiting for transfers between devices  327 us (57%)
  starting transfers between devices  118 us (20%)
  local copies, waits for them, and re-layouts  53.4 us (9%)
  matrix products  38.6 us (7%)
  other arithmetic  31.4 us (5%)
    ppermute x32, waiting for transfers between devices, passed_along(): return lax.ppermute(block, axis, route)  285 us
    ppermute x32, starting transfers between devices, passed_along(): return lax.ppermute(block, axis, route)  66.5 us
    all_to_all x1, starting transfers between devices, local(): lax.all_to_all(y_tan, 'head', split_axis=0, concat_axis=1, tiled=True)  39.4 us
    all_to_all x1, waiting for transfers between devices, local(): lax.all_to_all(y_tan, 'head', split_axis=0, concat_axis=1, tiled=True)  24.6 us
    all_to_all x1, waiting for transfers between devices, local(): lax.all_to_all(y_main, 'head', split_axis=0, concat_axis=1, tiled=True)  17.2 us
  transfers between devices with their start and end apart: 35, of which 33 were waited for; matrix products, arithmetic and copies ran while one was open for 18% of the time, Pallas kernels for 0%

commit v1 on v0

v1 whole, which is shorter than its diff:
```python
import functools

import jax
import jax.numpy as jnp
from jax import lax
from jax.experimental import pallas as pl
from jax.experimental.pallas import tpu as pltpu
from jax.sharding import PartitionSpec as P

Q = 256
HALF = 128
LANES = 128
PACK = 8
LOG2E = 1.4426950408889634
VMEM_BYTES = 48 * 1024 * 1024
F32 = jnp.float32
BF16 = jnp.bfloat16


def column_of(values):
    place = lax.broadcasted_iota(jnp.int32, (PACK, 1), 0)
    column = jnp.zeros((PACK, 1), F32)
    for h, value in enumerate(values):
        column = jnp.where(place == h, value, column)
    return column


def by_head(per_head, rows):
    low = lax.broadcasted_iota(jnp.int32, (rows, LANES), 1) < LANES // 2
    first = jnp.where(low, per_head[0], per_head[1])
    second = jnp.where(low, per_head[2], per_head[3])
    last = jnp.broadcast_to(per_head[4], (rows, LANES))
    return [first, first, second, second, last]


def head_tiles(main, tan):
    return [
        main[:, 0:128],
        tan[:, 0:128],
        main[:, 128:256],
        tan[:, 128:256],
        jnp.concatenate([main[:, 256:320], tan[:, 256:320]], axis=1),
    ]


def split_bf16(x, parts):
    pieces = []
    for _ in range(parts):
        piece = x.astype(BF16)
        pieces.append(piece)
        x = x - piece.astype(F32)
    return pieces


def state_kernel(
    heads, blocks, dt_bias, a_rate, traj, xs, dxs, bmat, dt_raw, rows, cols, local_in, fin, send
):
    bias = column_of([dt_bias[h] for h in range(heads)])
    rate = column_of([a_rate[h] * LOG2E for h in range(heads)])
    raw = jnp.concatenate([dt_raw[...], jnp.zeros((PACK - heads, blocks * Q), F32)], axis=0)
    pre = jnp.concatenate([raw[:, c * Q : (c + 1) * Q] for c in range(blocks)], axis=0)
    bias_all = jnp.concatenate([bias] * blocks, axis=0)
    rate_all = jnp.concatenate([rate] * blocks, axis=0)
    pre = pre + bias_all
    step = jnp.maximum(pre, 0.0) + jnp.log1p(jnp.exp(-jnp.abs(pre)))
    upper = (
        lax.broadcasted_iota(jnp.int32, (Q, Q), 0) <= lax.broadcasted_iota(jnp.int32, (Q, Q), 1)
    ).astype(BF16)
    logs = jnp.zeros((blocks * PACK, Q), F32)
    for piece in split_bf16(-(step * rate_all), 3)[::-1]:
        logs = logs + jnp.dot(piece, upper, preferred_element_type=F32)
    shifted = logs - jnp.log2(step)
    rows[...] = shifted
    ends = logs[:, Q - 1 : Q]
    weight_in = jnp.exp2(ends - shifted)
    end_decay = jnp.exp2(ends)

    state = jnp.zeros((LANES, heads * LANES), F32)
    factor = [jnp.ones((1, 1), F32)] * heads
    for c in range(blocks):
        at = slice(c * PACK, (c + 1) * PACK)
        table = jnp.concatenate(
            [weight_in[at], logs[at], jnp.zeros((LANES - 2 * PACK, Q), F32)], axis=0
        ).T
        here = slice(c * Q, (c + 1) * Q)
        cols[here, :] = table
        if c > 0:
            keep = jnp.where(traj[c] == traj[c - 1], 1.0, 0.0)
            state = state * keep
            factor = [f * keep for f in factor]
        local_in[c] = state.astype(BF16)
        fin[c : c + 1, :] = jnp.concatenate(by_head(factor, 1), axis=1)
        scale = by_head([table[:, h : h + 1] for h in range(heads)], Q)
        tiles = head_tiles(xs[here, :], dxs[here, :])
        weighted = jnp.concatenate(
            [(t.astype(F32) * s).astype(BF16) for t, s in zip(tiles, scale)], axis=1
        )
        gained = lax.dot_general(
            bmat[here, :], weighted, (((0,), (0,)), ((), ())), preferred_element_type=F32
        )
        ended = [end_decay[c * PACK + h : c * PACK + h + 1, :] for h in range(heads)]
        state = state * jnp.concatenate(by_head(ended, 1), axis=1) + gained
        factor = [f * e for f, e in zip(factor, ended)]
    fin[blocks:PACK, :] = jnp.zeros((PACK - blocks, heads * LANES), F32)
    lane = lax.broadcasted_iota(jnp.int32, (1, LANES), 1)
    notes = jnp.zeros((1, LANES), F32)
    for h in range(heads):
        rest = factor[h]
        for k in range(3):
            piece = rest.astype(BF16).astype(F32)
            notes = jnp.where(lane == k * heads + h, piece, notes)
            rest = rest - piece
    notes = jnp.where(lane == 3 * heads, traj[0].astype(F32), notes)
    notes = jnp.where(lane == 3 * heads + 1, traj[blocks - 1].astype(F32), notes)
    send[:, : heads * LANES] = state.astype(BF16)
    send[:, heads * LANES :] = jnp.broadcast_to(notes, (LANES, LANES)).astype(BF16)


def scan_kernel(heads, count, got, back, hold):
    width = heads * LANES
    everything = got[...].astype(F32)
    carried = jnp.zeros((PACK, width), F32)
    last_id = None
    for s in range(count):
        at = slice(s * PACK, (s + 1) * PACK)
        notes = everything[at, width:]
        factor = []
        for h in range(heads):
            total = notes[:, h : h + 1]
            for k in range(1, 3):
                total = total + notes[:, k * heads + h : k * heads + h + 1]
            factor.append(total)
        first_id = notes[:, 3 * heads : 3 * heads + 1]
        if s > 0:
            carried = jnp.where(first_id == last_id, carried, 0.0)
        hold[at, :] = carried
        last_id = notes[:, 3 * heads + 1 : 3 * heads + 2]
        carried = jnp.concatenate(by_head(factor, PACK), axis=1) * carried + everything[at, :width]
    back[...] = hold[...].astype(BF16)


def diagonal_kernel(heads, d_skip, xs, dxs, bmat, cmat, rows, cols, local_in, out):
    scores = lax.dot_general(
        cmat[...], bmat[...], (((1,), (1,)), ((), ())), preferred_element_type=F32
    )
    causal = lax.broadcasted_iota(jnp.int32, (HALF, HALF), 0) >= lax.broadcasted_iota(
        jnp.int32, (HALF, HALF), 1
    )
    tiles = head_tiles(xs[...], dxs[...])
    operands = [
        jnp.concatenate(tiles[0:2], axis=1),
        jnp.concatenate(tiles[2:4], axis=1),
        tiles[4],
    ]
    low = lax.broadcasted_iota(jnp.int32, (Q, LANES), 1) < LANES // 2
    sums = []
    for h in range(heads):
        log_t = cols[:, PACK + h : PACK + h + 1]
        log_s = rows[h : h + 1, :]
        near = jnp.where(
            causal, scores[:HALF, :HALF] * jnp.exp2(log_t[:HALF] - log_s[:, :HALF]), 0.0
        )
        far = scores[HALF:, :HALF] * jnp.exp2(log_t[HALF:] - log_s[:, :HALF])
        last = jnp.where(
            causal, scores[HALF:, HALF:] * jnp.exp2(log_t[HALF:] - log_s[:, HALF:]), 0.0
        )
        operand = operands[h // 2]
        top = jnp.dot(near.astype(BF16), operand[:HALF], preferred_element_type=F32)
        low_rows = jnp.concatenate([far, last], axis=1).astype(BF16)
        bottom = jnp.dot(low_rows, operand, preferred_element_type=F32)
        sums.append(jnp.concatenate([top, bottom], axis=0))
    diagonal = []
    for pair in range(heads // 2):
        left, right = sums[2 * pair], sums[2 * pair + 1]
        diagonal.append(jnp.where(low, left[:, :LANES], right[:, :LANES]))
        diagonal.append(jnp.where(low, left[:, LANES:], right[:, LANES:]))
    diagonal.append(sums[heads - 1])
    carried = jnp.dot(cmat[...], local_in[0], preferred_element_type=F32)
    decay = by_head([jnp.exp2(cols[:, PACK + h : PACK + h + 1]) for h in range(heads)], Q)
    skip = by_head([d_skip[h] for h in range(heads)], 1)
    for i in range(heads):
        at = slice(i * LANES, (i + 1) * LANES)
        out[:, at] = (
            diagonal[i] + carried[:, at] * decay[i] + tiles[i].astype(F32) * skip[i]
        )


def gate_kernel(heads, y_local, zgate, cmat, cols, fin, incoming, out):
    block = pl.program_id(0)
    carried = jnp.dot(cmat[...], incoming[...], preferred_element_type=F32)
    decay = by_head([jnp.exp2(cols[:, PACK + h : PACK + h + 1]) for h in range(heads)], Q)
    through = fin[pl.ds(block, 1), :]
    gates = head_tiles(zgate[...], zgate[...])
    for i in range(heads):
        at = slice(i * LANES, (i + 1) * LANES)
        gate = gates[i].astype(F32)
        y = y_local[:, at] + carried[:, at] * (decay[i] * through[:, at])
        out[:, at] = (y * (gate / (1.0 + jnp.exp(-gate)))).astype(BF16)


def norm_kernel(heads, sources, total_width, gathered, gain, normed, normed_tan):
    main_parts, tan_parts = [], []
    half = LANES // 2
    for s in range(sources):
        tiles = [
            gathered[s, :, i * LANES : (i + 1) * LANES].astype(F32) for i in range(heads)
        ]
        main_parts += [tiles[0], tiles[2], tiles[4][:, :half]]
        tan_parts += [tiles[1], tiles[3], tiles[4][:, half:]]
    width = heads * half
    mains, tans = [], []
    for s in range(0, sources, 2):
        mains.append(jnp.concatenate(main_parts[3 * s : 3 * s + 6], axis=1))
        tans.append(jnp.concatenate(tan_parts[3 * s : 3 * s + 6], axis=1))
    square = sum(jnp.sum(m * m, axis=1, keepdims=True) for m in mains)
    cross = sum(jnp.sum(m * t, axis=1, keepdims=True) for m, t in zip(mains, tans))
    mean_square = square / total_width
    mean_cross = cross / total_width
    inv_rms = lax.rsqrt(mean_square + 1e-05)
    pull = inv_rms * inv_rms * inv_rms * mean_cross
    for i, (m, t) in enumerate(zip(mains, tans)):
        at = slice(i * 2 * width, (i + 1) * 2 * width)
        g = gain[:, at]
        normed[:, at] = (g * m * inv_rms).astype(BF16)
        normed_tan[:, at] = (g * (t * inv_rms - m * pull)).astype(BF16)


def whole(shape):
    return pl.BlockSpec(shape, lambda *_: (0,) * len(shape))


SMEM_SPEC = pl.BlockSpec(memory_space=pltpu.SMEM)


def local(xs, dxs, zgate, bmat, cmat, dt_raw, dt_bias, a_rate, d_skip, gain, traj_ids):
    tokens, inner = xs.shape
    heads = dt_raw.shape[0]
    blocks = tokens // Q
    wide = heads * LANES
    state_rows = bmat.shape[1]
    sources = lax.axis_size("head")
    seq_size = lax.axis_size("seq")
    group = state_rows // PACK
    groups = [list(range(g, g + group)) for g in range(0, seq_size, group)]
    params = pltpu.CompilerParams(vmem_limit_bytes=VMEM_BYTES)

    rows, cols, local_in, fin, send = pl.pallas_call(
        functools.partial(state_kernel, heads, blocks),
        out_shape=(
            jax.ShapeDtypeStruct((blocks * PACK, Q), F32),
            jax.ShapeDtypeStruct((tokens, LANES), F32),
            jax.ShapeDtypeStruct((blocks, state_rows, wide), BF16),
            jax.ShapeDtypeStruct((PACK, wide), F32),
            jax.ShapeDtypeStruct((state_rows, wide + LANES), BF16),
        ),
        in_specs=[SMEM_SPEC] * 3 + [pl.BlockSpec(memory_space=pltpu.VMEM)] * 4,
        compiler_params=params,
        cost_estimate=pl.CostEstimate(
            flops=300_000_000, bytes_accessed=4_000_000, transcendentals=30_000
        ),
    )(dt_bias, a_rate, traj_ids, xs, dxs, bmat, dt_raw)

    got = lax.all_to_all(
        send, "seq", split_axis=0, concat_axis=0, tiled=True, axis_index_groups=groups
    )
    back = pl.pallas_call(
        functools.partial(scan_kernel, heads, group),
        out_shape=jax.ShapeDtypeStruct((state_rows, wide), BF16),
        scratch_shapes=[pltpu.VMEM((state_rows, wide), F32)],
        compiler_params=params,
    )(got)
    incoming = lax.all_to_all(
        back, "seq", split_axis=0, concat_axis=0, tiled=True, axis_index_groups=groups
    )

    def token_block(width):
        return pl.BlockSpec((Q, width), lambda c: (c, 0))

    y_local = pl.pallas_call(
        functools.partial(diagonal_kernel, heads),
        grid=(blocks,),
        out_shape=jax.ShapeDtypeStruct((tokens, wide), F32),
        in_specs=[
            SMEM_SPEC,
            token_block(inner),
            token_block(inner),
            token_block(state_rows),
            token_block(state_rows),
            pl.BlockSpec((PACK, Q), lambda c: (c, 0)),
            token_block(LANES),
            pl.BlockSpec((1, state_rows, wide), lambda c: (c, 0, 0)),
        ],
        out_specs=token_block(wide),
        compiler_params=params,
        cost_estimate=pl.CostEstimate(
            flops=1_500_000_000, bytes_accessed=8_000_000, transcendentals=2_000_000
        ),
    )(d_skip, xs, dxs, bmat, cmat, rows, cols, local_in)

    gated = pl.pallas_call(
        functools.partial(gate_kernel, heads),
        grid=(blocks,),
        out_shape=jax.ShapeDtypeStruct((tokens, wide), BF16),
        in_specs=[
            token_block(wide),
            token_block(inner),
            token_block(state_rows),
            token_block(LANES),
            whole((PACK, wide)),
            whole((state_rows, wide)),
        ],
        out_specs=token_block(wide),
        compiler_params=params,
        cost_estimate=pl.CostEstimate(
            flops=260_000_000, bytes_accessed=8_000_000, transcendentals=500_000
        ),
    )(y_local, zgate, cmat, cols, fin, incoming)

    gathered = lax.all_to_all(gated, "head", split_axis=0, concat_axis=0, tiled=True)
    mine = tokens // sources
    strip = 16
    total = inner * sources
    return pl.pallas_call(
        functools.partial(norm_kernel, heads, sources, float(total)),
        grid=(mine // strip,),
        out_shape=(
            jax.ShapeDtypeStruct((mine, total), BF16),
            jax.ShapeDtypeStruct((mine, total), BF16),
        ),
        in_specs=[
            pl.BlockSpec((sources, strip, wide), lambda i: (0, i, 0)),
            whole((1, total)),
        ],
        out_specs=(
            pl.BlockSpec((strip, total), lambda i: (i, 0)),
            pl.BlockSpec((strip, total), lambda i: (i, 0)),
        ),
        compiler_params=params,
    )(gathered.reshape(sources, mine, wide), gain.reshape(1, total))


def solution(mesh):
    placed = (
        P("seq", "head"),
        P("seq", "head"),
        P("seq", "head"),
        P("seq", None),
        P("seq", None),
        P("head", "seq"),
        P("head"),
        P("head"),
        P("head"),
        P(),
        P("seq"),
    )
    return jax.shard_map(
        local,
        mesh=mesh,
        in_specs=placed,
        out_specs=(P(("seq", "head"), None), P(("seq", "head"), None)),
        check_vma=False,
    )
```

time: 576 us -> 116 us (0.20)
  waiting for transfers between devices: 327 us -> 0.01 us
  starting transfers between devices: 118 us -> 5.71 us
  blocking collectives: 0 us -> 75 us
  matrix products: 38.6 us -> 0 us
  local copies, waits for them, and re-layouts: 53.4 us -> 15.5 us
  other arithmetic: 31.4 us -> 0 us
  Pallas kernels: 0 us -> 17.7 us
    ppermute x32 -> x0, waiting for transfers between devices: 285 us -> none  [passed_along(): return lax.ppermute(block, axis, route)]
    all_to_all x0 -> x2, blocking collectives: none -> 75 us  [the longest x1 56.8 us: local(): lax.all_to_all(gated, 'head', split_axis=0, concat_axis=0, tiled=True)]
    ppermute x32 -> x0, starting transfers between devices: 66.5 us -> none  [passed_along(): return lax.ppermute(block, axis, route)]
    all_to_all x3 -> x1, starting transfers between devices: 52 us -> 5.71 us  [local(): lax.all_to_all(back, 'seq', split_axis=0, concat_axis=0, tiled=True, axis...]
    all_to_all x3 -> x1, waiting for transfers between devices: 41.9 us -> 0.01 us  [local(): lax.all_to_all(back, 'seq', split_axis=0, concat_axis=0, tiled=True, axis...]
    dot_general x25 -> x0, matrix products: 38.6 us -> none  [the longest x6 10.3 us: local_block(): jnp.einsum('shp,sn->hpn', weighted, b_block, preferred_element_type=jnp.f...]
    convert_element_type x7 -> x0, local copies, waits for them, and re-layouts: 20.2 us -> none  [the longest x2 5.79 us: gate_rows(): y_main.astype(jnp.float32) * gate_value]
    pallas_call x0 -> x5, Pallas kernels: none -> 17.7 us  [the longest x1 5.49 us: local(): pl.pallas_call(functools.partial(diagonal_kernel, heads), grid=(blocks,),...]
  transfers between devices with their start and end apart: 35 -> 1, of which waited for: 33 -> 0; matrix products, arithmetic and copies ran while one was open for 18% -> 1% of each run, Pallas kernels for 0% -> 5%
where the time goes in v1:
time: 116 us; the launch traced here: 115 us
  blocking collectives  75 us (65%)
  Pallas kernels  17.7 us (15%)
  local copies, waits for them, and re-layouts  15.5 us (13%)
  starting transfers between devices  5.71 us (5%)
    all_to_all x1, blocking collectives, local(): lax.all_to_all(gated, 'head', split_axis=0, concat_axis=0, tiled=True)  56.8 us
    all_to_all x1, blocking collectives, local(): lax.all_to_all(send, 'seq', split_axis=0, concat_axis=0, tiled=True, axis...  18.2 us
    unnamed x41, local copies, waits for them, and re-layouts  15.5 us
    all_to_all x1, starting transfers between devices, local(): lax.all_to_all(back, 'seq', split_axis=0, concat_axis=0, tiled=True, axis...  5.71 us
    pallas_call x1, Pallas kernels, local(): pl.pallas_call(functools.partial(diagonal_kernel, heads), grid=(blocks,),...  5.49 us
    pallas_call x1, Pallas kernels, local(): pl.pallas_call(functools.partial(gate_kernel, heads), grid=(blocks,), out...  4.79 us
    pallas_call x1, Pallas kernels, local(): pl.pallas_call(functools.partial(norm_kernel, heads, sources, float(total...  3.35 us
    pallas_call x1, Pallas kernels, local(): pl.pallas_call(functools.partial(state_kernel, heads, blocks), out_shape=...  2.9 us
  transfers between devices with their start and end apart: 1, of which 0 were waited for; matrix products, arithmetic and copies ran while one was open for 1% of the time, Pallas kernels for 5%

profile of v1, /device:TPU:7, one launch (start us, length us, event | category | flops | bytes accessed | tf_op | source)
XLA Modules:
  0.0 114.7 jit_solution(4810569190574800260)
XLA Ops:
  0.6 0.0 copy-start.3
  0.6 0.0 copy-start.11
  0.7 0.0 copy-start.16
  0.7 0.0 copy-start.17
  0.7 0.0 copy-start.18
  0.7 1.7 %copy.15.xs = bf16[1536,320]{1,0:T(8,128)(2,1)S(1)} copy(bf16[1536,320]{0,1:T(8,128)(2,1)} %param.11) | data formatting | bytes 1966080 | tf_op args[0]
  2.4 1.7 %copy.16.dxs = bf16[1536,320]{1,0:T(8,128)(2,1)S(1)} copy(bf16[1536,320]{0,1:T(8,128)(2,1)} %param.12) | data formatting | bytes 1966080 | tf_op args[1]
  4.1 0.0 copy-done.3
  4.1 2.9 %shard_map.122 = (f32[48,256]{1,0:T(8,128)S(1)}, f32[1536,128]{1,0:T(8,128)S(1)}, bf16[6,128,640]{2,1,0:T(8,128)(2,1)S(1)}, f32[8,640]{1,0:T(8,128)S(1)}, bf16[128,768]{1,0:T(8,128)(2,1)S(1)}) custom-call(f32[5]{0:T(128)S(1)} %copy-done.16, f32[5]{0:T(128)S(1)} %copy-done.17, s32[6]{0:T(128)S(1)} %copy-done.18, bf16[1536,320]{1,0:T(8,128)(2,1)S(1)} %copy.15.xs, ...), custom_call_target="tpu_custom_call" | custom-call | flops 300000000 | bytes 4000000 | tf_op jit(solution)/shard_map/pallas_call | solution.py:247
  7.0 0.0 copy-start
  7.0 0.9 copy-done
  7.9 0.9 copy-done.7
  8.9 0.6 copy-done.13
  9.5 18.2 %all_to_all.31 = bf16[16,8,768]{2,1,0:T(8,128)(2,1)S(1)} all-to-all(bf16[16,8,768]{2,1,0:T(8,128)(2,1)S(1)} %bitcast.8), channel_id=1, replica_groups={{0,16,32,48,64,80,96,112,128,144,160,176,192,208,224,240},{256,272,288,..., dimensions={0} | all-to-all | bytes 393216 | tf_op jit(solution)/shard_map/all_to_all | solution.py:263
  27.6 1.2 %shard_map.124 = bf16[128,640]{1,0:T(8,128)(2,1)} custom-call(bf16[128,768]{1,0:T(8,128)(2,1)S(1)} %bitcast.7), custom_call_target="tpu_custom_call" | custom-call | tf_op jit(solution)/shard_map/pallas_call | solution.py:266
  28.8 5.7 %all-to-all-start.1 = ((bf16[16,8,640]{2,1,0:T(8,128)(2,1)}), bf16[16,8,640]{2,1,0:T(8,128)(2,1)}, u32[]{:S(2)}, u32[]{:S(2)}) async-start(bf16[16,8,640]{2,1,0:T(8,128)(2,1)} %bitcast.2), calls=%async_computation.1 | async-start | bytes 327680 | tf_op jit(solution)/shard_map/all_to_all | solution.py:272
  34.5 1.7 %copy.17.zgate = bf16[1536,320]{1,0:T(8,128)(2,1)S(1)} copy(bf16[1536,320]{0,1:T(8,128)(2,1)} %param.13) | data formatting | bytes 1966080 | tf_op args[2]
  36.2 0.0 copy-start.1
  36.2 1.1 copy-done.1
  37.3 1.0 copy-done.4
  38.3 1.0 copy-done.5
  39.3 1.2 %copy-done.8 = bf16[6,128,640]{2,1,0:T(8,128)(2,1)S(1)} copy-done((bf16[6,128,640]{2,1,0:T(8,128)(2,1)S(1)}, bf16[6,128,640]{2,1,0:T(8,128)(2,1)}, u32[]{:S(2)}) %copy-start.8) | copy-done | bytes 983064
  40.5 0.8 copy-done.10
  41.3 5.5 %shard_map.123.y_local = f32[1536,640]{1,0:T(8,128)} custom-call(f32[5]{0:T(128)S(1)} %copy-done.15, bf16[1536,320]{1,0:T(8,128)(2,1)S(1)} %copy.15.xs, bf16[1536,320]{1,0:T(8,128)(2,1)S(1)} %copy.16.dxs, bf16[1536,128]{1,0:T(8,128)(2,1)S(1)} %copy-done.4, bf16[1536,128]{1,0:T(8,128)(2,1)S(1)} %copy-done.5, f32[48,256]{1,0:T(8,128)S(1)} %copy-done.10, ...), custom_call_target="tpu_custom_call" | custom-call | flops 1500000000 | bytes 8000000 | tf_op jit(solution)/shard_map/pallas_call | solution.py:279
  46.8 0.0 all-to-all-done.1
  46.8 1.1 copy-done.2
  48.0 1.0 copy-done.6
  49.0 0.7 copy-done.14
  49.7 4.8 %shard_map.125 = bf16[1536,640]{1,0:T(8,128)(2,1)S(1)} custom-call(f32[1536,640]{1,0:T(8,128)} %shard_map.123.y_local, bf16[1536,320]{1,0:T(8,128)(2,1)S(1)} %copy.17.zgate, bf16[1536,128]{1,0:T(8,128)(2,1)S(1)} %copy-done.6, f32[1536,128]{1,0:T(8,128)S(1)} %copy-done.2, f32[8,640]{1,0:T(8,128)S(1)} %copy-done.14, bf16[128,640]{1,0:T(8,128)(2,1)} %bitcast.3.incoming), custom_call_target="tpu_custom_call" | custom-call | flops 260000000 | bytes 8000000 | tf_op jit(solution)/shard_map/pallas_call | solution.py:300
  54.5 0.0 copy-start.12
  54.5 56.8 %all_to_all.32.gathered = bf16[16,96,640]{2,1,0:T(8,128)(2,1)S(1)} all-to-all(bf16[16,96,640]{2,1,0:T(8,128)(2,1)S(1)} %bitcast.6), channel_id=1, replica_groups=mesh['seq'=32,'head'=16] {'head'}, dimensions={0} | all-to-all | bytes 3932160 | tf_op jit(solution)/shard_map/all_to_all | solution.py:319
  111.3 3.3 %shard_map.126 = (bf16[96,5120]{1,0:T(8,128)(2,1)}, bf16[96,5120]{1,0:T(8,128)(2,1)}) custom-call(bf16[16,96,640]{2,1,0:T(8,128)(2,1)S(1)} %all_to_all.32.gathered, f32[1,5120]{1,0:T(1,128)S(1)} %bitcast.9), custom_call_target="tpu_custom_call" | custom-call | tf_op jit(solution)/shard_map/pallas_call | solution.py:323
  (18 shorter events, 0.0 us)
Async XLA Ops:
  0.6 3.4 %copy-start.3 = (bf16[1536,128]{1,0:T(8,128)(2,1)S(1)}, bf16[1536,128]{1,0:T(8,128)(2,1)}, u32[]{:S(2)}) copy-start(bf16[1536,128]{1,0:T(8,128)(2,1)} %bmat.3) | copy-start | bytes 1179652
  0.6 3.4 %copy-start.11 = (f32[5,1536]{1,0:T(8,128)S(1)}, f32[5,1536]{1,0:T(8,128)}, u32[]{:S(2)}) copy-start(f32[5,1536]{1,0:T(8,128)} %dt_raw.1) | copy-start | bytes 92164
  0.7 3.4 %copy-start.16 = (f32[5]{0:T(128)S(1)}, f32[5]{0:T(128)}, u32[]{:S(2)}) copy-start(f32[5]{0:T(128)} %dt_bias.1) | copy-start | bytes 64
  0.7 3.4 %copy-start.17 = (f32[5]{0:T(128)S(1)}, f32[5]{0:T(128)}, u32[]{:S(2)}) copy-start(f32[5]{0:T(128)} %a_rate.1) | copy-start | bytes 64
  0.7 3.4 %copy-start.18 = (s32[6]{0:T(128)S(1)}, s32[6]{0:T(128)}, u32[]{:S(2)}) copy-start(s32[6]{0:T(128)} %traj.1) | copy-start | bytes 76
  7.0 0.9 copy-start
  7.9 0.9 copy-start.7
  8.9 0.6 copy-start.13
  9.5 19.3 %copy-start.9 = (f32[48,256]{1,0:T(8,128)}, f32[48,256]{1,0:T(8,128)S(1)}, u32[]{:S(2)}) copy-start(f32[48,256]{1,0:T(8,128)S(1)} %get-tuple-element.7.rows) | copy-start | bytes 147460
  9.5 26.7 %copy-start.15 = (f32[5]{0:T(128)S(1)}, f32[5]{0:T(128)}, u32[]{:S(2)}) copy-start(f32[5]{0:T(128)} %d_skip.1) | copy-start | bytes 64
  28.8 18.0 %all-to-all-start.1 = ((bf16[16,8,640]{2,1,0:T(8,128)(2,1)}), bf16[16,8,640]{2,1,0:T(8,128)(2,1)}, u32[]{:S(2)}, u32[]{:S(2)}) async-start(bf16[16,8,640]{2,1,0:T(8,128)(2,1)} %bitcast.2), calls=%async_computation.1 | async-start | bytes 327680 | tf_op jit(solution)/shard_map/all_to_all | solution.py:272
  36.2 1.1 copy-start.1
  37.3 1.0 copy-start.4
  38.3 1.0 copy-start.5
  39.3 1.2 %copy-start.8 = (bf16[6,128,640]{2,1,0:T(8,128)(2,1)S(1)}, bf16[6,128,640]{2,1,0:T(8,128)(2,1)}, u32[]{:S(2)}) copy-start(bf16[6,128,640]{2,1,0:T(8,128)(2,1)} %copy-done.7) | copy-start | bytes 2949124
  40.5 0.8 copy-start.10
  46.8 1.1 copy-start.2
  48.0 1.0 copy-start.6
  49.0 0.7 copy-start.14
  54.5 56.9 %copy-start.12 = (f32[5120]{0:T(1024)S(1)}, f32[5120]{0:T(1024)}, u32[]{:S(2)}) copy-start(f32[5120]{0:T(1024)} %param.20) | copy-start | bytes 61444

commit v2 on v1

v2 whole, which is shorter than its diff:
```python
import functools

import jax
import jax.numpy as jnp
from jax import lax
from jax.experimental import pallas as pl
from jax.experimental.pallas import tpu as pltpu
from jax.sharding import PartitionSpec as P

Q = 256
HALF = 128
LANES = 128
PACK = 8
LOG2E = 1.4426950408889634
MIB = 1024 * 1024
F32 = jnp.float32
BF16 = jnp.bfloat16


def column_of(values):
    place = lax.broadcasted_iota(jnp.int32, (PACK, 1), 0)
    column = jnp.zeros((PACK, 1), F32)
    for h, value in enumerate(values):
        column = jnp.where(place == h, value, column)
    return column


def by_head(per_head, rows):
    low = lax.broadcasted_iota(jnp.int32, (rows, LANES), 1) < LANES // 2
    first = jnp.where(low, per_head[0], per_head[1])
    second = jnp.where(low, per_head[2], per_head[3])
    last = jnp.broadcast_to(per_head[4], (rows, LANES))
    return [first, first, second, second, last]


def feature_rows(main, tan, heads, width):
    order = []
    for pair in range(0, heads, 2):
        for array in (main, tan):
            for h in range(pair, min(pair + 2, heads)):
                order.append((h, array[h * width : (h + 1) * width, :]))
    return order


def split_bf16(x, parts):
    pieces = []
    for _ in range(parts):
        piece = x.astype(BF16)
        pieces.append(piece)
        x = x - piece.astype(F32)
    return pieces


def across(left, right):
    return lax.dot_general(left, right, (((1,), (1,)), ((), ())), preferred_element_type=F32)


def state_kernel(
    heads,
    blocks,
    dt_bias,
    a_rate,
    traj,
    dt_raw,
    xs_hbm,
    dxs_hbm,
    bmat_hbm,
    shifted_out,
    logs_out,
    local_out,
    fin,
    send,
    xs,
    dxs,
    bmat,
    local_in,
    sems,
    out_sems,
):
    copies = [
        pltpu.make_async_copy(source, target, sems.at[i])
        for i, (source, target) in enumerate(
            ((xs_hbm, xs), (dxs_hbm, dxs), (bmat_hbm, bmat))
        )
    ]
    for copy in copies:
        copy.start()
    width = xs.shape[0] // heads
    bias = column_of([dt_bias[h] for h in range(heads)])
    rate = column_of([a_rate[h] * LOG2E for h in range(heads)])
    raw = jnp.concatenate([dt_raw[...], jnp.zeros((PACK - heads, blocks * Q), F32)], axis=0)
    pre = jnp.concatenate([raw[:, c * Q : (c + 1) * Q] for c in range(blocks)], axis=0)
    pre = pre + jnp.concatenate([bias] * blocks, axis=0)
    step = jnp.maximum(pre, 0.0) + jnp.log1p(jnp.exp(-jnp.abs(pre)))
    upper = (
        lax.broadcasted_iota(jnp.int32, (Q, Q), 0) <= lax.broadcasted_iota(jnp.int32, (Q, Q), 1)
    ).astype(BF16)
    logs = jnp.zeros((blocks * PACK, Q), F32)
    for piece in split_bf16(-(step * jnp.concatenate([rate] * blocks, axis=0)), 3)[::-1]:
        logs = logs + jnp.dot(piece, upper, preferred_element_type=F32)
    shifted = logs - jnp.log2(step)
    shifted_out[...] = shifted
    logs_out[...] = logs
    ends = logs[:, Q - 1 : Q]
    weight_in = jnp.exp2(ends - shifted)
    end_decay = jnp.exp2(ends)

    for copy in copies:
        copy.wait()
    state = jnp.zeros((LANES, heads * LANES), F32)
    factor = jnp.ones((PACK, 1), F32)
    copies_out = []
    for c in range(blocks):
        here = slice(c * Q, (c + 1) * Q)
        if c > 0:
            keep = jnp.where(traj[c] == traj[c - 1], 1.0, 0.0)
            state = state * keep
            factor = factor * keep
        local_in[c] = state.astype(BF16)
        leaving = pltpu.make_async_copy(local_in.at[c], local_out.at[c], out_sems.at[c])
        leaving.start()
        copies_out.append(leaving)
        fin[c * PACK : (c + 1) * PACK, :] = jnp.broadcast_to(factor, (PACK, LANES))
        weighted = jnp.concatenate(
            [
                (part.astype(F32) * weight_in[c * PACK + h : c * PACK + h + 1, :]).astype(BF16)
                for h, part in feature_rows(xs[:, here], dxs[:, here], heads, width)
            ],
            axis=0,
        )
        gained = across(bmat[here, :].T, weighted)
        ended = end_decay[c * PACK : (c + 1) * PACK, :]
        decay = by_head([ended[h : h + 1, :] for h in range(heads)], 1)
        state = state * jnp.concatenate(decay, axis=1) + gained
        factor = factor * ended
    lane = lax.broadcasted_iota(jnp.int32, (1, LANES), 1)
    notes = jnp.zeros((1, LANES), F32)
    for h in range(heads):
        rest = factor[h : h + 1, :]
        for k in range(3):
            piece = rest.astype(BF16).astype(F32)
            notes = jnp.where(lane == k * heads + h, piece, notes)
            rest = rest - piece
    notes = jnp.where(lane == 3 * heads, traj[0].astype(F32), notes)
    notes = jnp.where(lane == 3 * heads + 1, traj[blocks - 1].astype(F32), notes)
    send[:, : heads * LANES] = state.astype(BF16)
    send[:, heads * LANES :] = jnp.broadcast_to(notes, (LANES, LANES)).astype(BF16)
    for leaving in copies_out:
        leaving.wait()


def scan_kernel(heads, count, got, _, back, hold):
    width = heads * LANES
    everything = got[...].astype(F32)
    carried = jnp.zeros((PACK, width), F32)
    last_id = None
    for s in range(count):
        at = slice(s * PACK, (s + 1) * PACK)
        notes = everything[at, width:]
        factor = []
        for h in range(heads):
            total = notes[:, h : h + 1]
            for k in range(1, 3):
                total = total + notes[:, k * heads + h : k * heads + h + 1]
            factor.append(total)
        first_id = notes[:, 3 * heads : 3 * heads + 1]
        if s > 0:
            carried = jnp.where(first_id == last_id, carried, 0.0)
        hold[at, :] = carried
        last_id = notes[:, 3 * heads + 1 : 3 * heads + 2]
        carried = jnp.concatenate(by_head(factor, PACK), axis=1) * carried + everything[at, :width]
    back[...] = hold[...].astype(BF16)


def diagonal_kernel(
    heads, d_skip, xs, dxs, bmat, cmat, shifted, logs, local_in, fin, y_local, reach, token
):
    width = xs.shape[0] // heads
    decays = jnp.exp2(logs[...])
    table = jnp.concatenate(
        [logs[...], decays, decays * fin[:, 0:1], jnp.zeros((LANES - 3 * PACK, Q), F32)], axis=0
    ).T
    reach[...] = table
    token[...] = table[:PACK, :]
    scores = across(cmat[...], bmat[...])
    causal = lax.broadcasted_iota(jnp.int32, (HALF, HALF), 0) >= lax.broadcasted_iota(
        jnp.int32, (HALF, HALF), 1
    )
    unit = (
        lax.broadcasted_iota(jnp.int32, (Q, Q), 0) == lax.broadcasted_iota(jnp.int32, (Q, Q), 1)
    ).astype(BF16)
    joined = jnp.concatenate(
        [part for _, part in feature_rows(xs[...], dxs[...], heads, width)], axis=0
    )
    plain = across(unit, joined)
    low = lax.broadcasted_iota(jnp.int32, (Q, LANES), 1) < LANES // 2
    sums = []
    for h in range(heads):
        log_t = table[:, h : h + 1]
        log_s = shifted[h : h + 1, :]
        near = jnp.where(
            causal, scores[:HALF, :HALF] * jnp.exp2(log_t[:HALF] - log_s[:, :HALF]), 0.0
        )
        far = scores[HALF:, :HALF] * jnp.exp2(log_t[HALF:] - log_s[:, :HALF])
        last = jnp.where(
            causal, scores[HALF:, HALF:] * jnp.exp2(log_t[HALF:] - log_s[:, HALF:]), 0.0
        )
        operand = joined[(h // 2) * 2 * LANES : (h // 2 + 1) * 2 * LANES]
        top = across(near.astype(BF16), operand[:, :HALF])
        bottom = across(jnp.concatenate([far, last], axis=1).astype(BF16), operand)
        sums.append(jnp.concatenate([top, bottom], axis=0))
    diagonal = []
    for pair in range(heads // 2):
        left, right = sums[2 * pair], sums[2 * pair + 1]
        diagonal.append(jnp.where(low, left[:, :LANES], right[:, :LANES]))
        diagonal.append(jnp.where(low, left[:, LANES:], right[:, LANES:]))
    diagonal.append(sums[heads - 1])
    carried = jnp.dot(cmat[...], local_in[0], preferred_element_type=F32)
    decay = by_head([table[:, PACK + h : PACK + h + 1] for h in range(heads)], Q)
    skip = by_head([d_skip[h] for h in range(heads)], 1)
    for i in range(heads):
        at = slice(i * LANES, (i + 1) * LANES)
        y_local[:, at] = diagonal[i] + carried[:, at] * decay[i] + plain[:, at] * skip[i]


def prepare_kernel(heads, zgate, y_local, reach, _, base, slope):
    unit = (
        lax.broadcasted_iota(jnp.int32, (Q, Q), 0) == lax.broadcasted_iota(jnp.int32, (Q, Q), 1)
    ).astype(BF16)
    z = across(unit, zgate[...])
    gate = z / (1.0 + jnp.exp(-z))
    gate_last = gate[:, 2 * LANES :]
    gates = [gate[:, :LANES], gate[:, LANES : 2 * LANES]]
    gates = [gates[0], gates[0], gates[1], gates[1]]
    gates.append(jnp.concatenate([gate_last, gate_last], axis=1))
    reached = by_head([reach[:, 2 * PACK + h : 2 * PACK + h + 1] for h in range(heads)], Q)
    for i in range(heads):
        at = slice(i * LANES, (i + 1) * LANES)
        base[:, at] = y_local[:, at] * gates[i]
        slope[:, at] = (reached[i] * gates[i]).astype(BF16)


def gate_kernel(base, slope, cmat, incoming, out):
    carried = jnp.dot(cmat[...], incoming[...], preferred_element_type=F32)
    out[...] = (base[...] + carried * slope[...].astype(F32)).astype(BF16)


def norm_kernel(heads, sources, total_width, gathered, gain, normed, normed_tan):
    main_parts, tan_parts = [], []
    half = LANES // 2
    for s in range(sources):
        tiles = [
            gathered[s, :, i * LANES : (i + 1) * LANES].astype(F32) for i in range(heads)
        ]
        main_parts += [tiles[0], tiles[2], tiles[4][:, :half]]
        tan_parts += [tiles[1], tiles[3], tiles[4][:, half:]]
    width = heads * half
    mains, tans = [], []
    for s in range(0, sources, 2):
        mains.append(jnp.concatenate(main_parts[3 * s : 3 * s + 6], axis=1))
        tans.append(jnp.concatenate(tan_parts[3 * s : 3 * s + 6], axis=1))
    square = sum(jnp.sum(m * m, axis=1, keepdims=True) for m in mains)
    cross = sum(jnp.sum(m * t, axis=1, keepdims=True) for m, t in zip(mains, tans))
    mean_square = square / total_width
    mean_cross = cross / total_width
    inv_rms = lax.rsqrt(mean_square + 1e-05)
    pull = inv_rms * inv_rms * inv_rms * mean_cross
    for i, (m, t) in enumerate(zip(mains, tans)):
        at = slice(i * 2 * width, (i + 1) * 2 * width)
        g = gain[:, at]
        normed[:, at] = (g * m * inv_rms).astype(BF16)
        normed_tan[:, at] = (g * (t * inv_rms - m * pull)).astype(BF16)


def whole(shape):
    return pl.BlockSpec(shape, lambda *_: (0,) * len(shape))


SMEM_SPEC = pl.BlockSpec(memory_space=pltpu.SMEM)


def local(xs, dxs, zgate, bmat, cmat, dt_raw, dt_bias, a_rate, d_skip, gain, traj_ids):
    tokens, inner = xs.shape
    heads = dt_raw.shape[0]
    blocks = tokens // Q
    wide = heads * LANES
    state_rows = bmat.shape[1]
    sources = lax.axis_size("head")
    seq_size = lax.axis_size("seq")
    group = state_rows // PACK
    groups = [list(range(g, g + group)) for g in range(0, seq_size, group)]
    params = pltpu.CompilerParams(vmem_limit_bytes=60 * MIB)
    small = pltpu.CompilerParams(vmem_limit_bytes=16 * MIB)
    roomy = pltpu.CompilerParams(vmem_limit_bytes=56 * MIB)
    in_vmem = pl.BlockSpec(memory_space=pltpu.VMEM)
    in_hbm = pl.BlockSpec(memory_space=pl.ANY)
    xs, dxs, zgate = xs.T, dxs.T, zgate.T

    shifted, logs, local_in, fin, send = pl.pallas_call(
        functools.partial(state_kernel, heads, blocks),
        out_shape=(
            jax.ShapeDtypeStruct((blocks * PACK, Q), F32),
            jax.ShapeDtypeStruct((blocks * PACK, Q), F32),
            jax.ShapeDtypeStruct((blocks, state_rows, wide), BF16),
            jax.ShapeDtypeStruct((blocks * PACK, LANES), F32),
            jax.ShapeDtypeStruct((state_rows, wide + LANES), BF16),
        ),
        in_specs=[SMEM_SPEC] * 3 + [in_vmem] + [in_hbm] * 3,
        out_specs=(in_vmem, in_vmem, in_hbm, in_vmem, in_vmem),
        scratch_shapes=[
            pltpu.VMEM((inner, tokens), BF16),
            pltpu.VMEM((inner, tokens), BF16),
            pltpu.VMEM((tokens, state_rows), BF16),
            pltpu.VMEM((blocks, state_rows, wide), BF16),
            pltpu.SemaphoreType.DMA((3,)),
            pltpu.SemaphoreType.DMA((blocks,)),
        ],
        compiler_params=params,
        cost_estimate=pl.CostEstimate(
            flops=300_000_000, bytes_accessed=4_000_000, transcendentals=30_000
        ),
    )(dt_bias, a_rate, traj_ids, dt_raw, xs, dxs, bmat)

    def token_block(width):
        return pl.BlockSpec((Q, width), lambda c: (c, 0))

    def feature_block(width):
        return pl.BlockSpec((width, Q), lambda c: (0, c))

    y_local, reach, token = pl.pallas_call(
        functools.partial(diagonal_kernel, heads),
        grid=(blocks,),
        out_shape=(
            jax.ShapeDtypeStruct((tokens, wide), F32),
            jax.ShapeDtypeStruct((tokens, LANES), F32),
            jax.ShapeDtypeStruct((PACK, LANES), F32),
        ),
        in_specs=[
            SMEM_SPEC,
            feature_block(inner),
            feature_block(inner),
            token_block(state_rows),
            token_block(state_rows),
            pl.BlockSpec((PACK, Q), lambda c: (c, 0)),
            pl.BlockSpec((PACK, Q), lambda c: (c, 0)),
            pl.BlockSpec((1, state_rows, wide), lambda c: (c, 0, 0)),
            pl.BlockSpec((PACK, LANES), lambda c: (c, 0)),
        ],
        out_specs=(token_block(wide), token_block(LANES), whole((PACK, LANES))),
        compiler_params=params,
        cost_estimate=pl.CostEstimate(
            flops=2_000_000_000, bytes_accessed=16_000_000, transcendentals=2_000_000
        ),
    )(d_skip, xs, dxs, bmat, cmat, shifted, logs, local_in, fin)

    got = lax.all_to_all(
        send, "seq", split_axis=0, concat_axis=0, tiled=True, axis_index_groups=groups
    )
    back = pl.pallas_call(
        functools.partial(scan_kernel, heads, group),
        out_shape=jax.ShapeDtypeStruct((state_rows, wide), BF16),
        in_specs=[in_vmem, in_hbm],
        scratch_shapes=[pltpu.VMEM((state_rows, wide), F32)],
        compiler_params=small,
    )(got, token)
    incoming = lax.all_to_all(
        back, "seq", split_axis=0, concat_axis=0, tiled=True, axis_index_groups=groups
    )
    base, slope = pl.pallas_call(
        functools.partial(prepare_kernel, heads),
        grid=(blocks,),
        out_shape=(
            jax.ShapeDtypeStruct((tokens, wide), F32),
            jax.ShapeDtypeStruct((tokens, wide), BF16),
        ),
        in_specs=[
            feature_block(inner),
            token_block(wide),
            token_block(LANES),
            in_hbm,
        ],
        out_specs=(token_block(wide), token_block(wide)),
        compiler_params=params,
        cost_estimate=pl.CostEstimate(
            flops=300_000_000, bytes_accessed=16_000_000, transcendentals=500_000
        ),
    )(zgate, y_local, reach, back)

    gated = pl.pallas_call(
        gate_kernel,
        grid=(blocks,),
        out_shape=jax.ShapeDtypeStruct((tokens, wide), BF16),
        in_specs=[
            token_block(wide),
            token_block(wide),
            token_block(state_rows),
            whole((state_rows, wide)),
        ],
        out_specs=token_block(wide),
        compiler_params=roomy,
        cost_estimate=pl.CostEstimate(
            flops=260_000_000, bytes_accessed=8_000_000, transcendentals=0
        ),
    )(base, slope, cmat, incoming)

    gathered = lax.all_to_all(gated, "head", split_axis=0, concat_axis=0, tiled=True)
    mine = tokens // sources
    strip = 16
    total = inner * sources
    return pl.pallas_call(
        functools.partial(norm_kernel, heads, sources, float(total)),
        grid=(mine // strip,),
        out_shape=(
            jax.ShapeDtypeStruct((mine, total), BF16),
            jax.ShapeDtypeStruct((mine, total), BF16),
        ),
        in_specs=[
            pl.BlockSpec((sources, strip, wide), lambda i: (0, i, 0)),
            whole((1, total)),
        ],
        out_specs=(
            pl.BlockSpec((strip, total), lambda i: (i, 0)),
            pl.BlockSpec((strip, total), lambda i: (i, 0)),
        ),
        compiler_params=params,
    )(gathered.reshape(sources, mine, wide), gain.reshape(1, total))


def solution(mesh):
    placed = (
        P("seq", "head"),
        P("seq", "head"),
        P("seq", "head"),
        P("seq", None),
        P("seq", None),
        P("head", "seq"),
        P("head"),
        P("head"),
        P("head"),
        P(),
        P("seq"),
    )
    return jax.shard_map(
        local,
        mesh=mesh,
        in_specs=placed,
        out_specs=(P(("seq", "head"), None), P(("seq", "head"), None)),
        check_vma=False,
    )
```

time: 116 us -> 113 us (0.974)
  blocking collectives: 75 us -> 57.7 us
  Pallas kernels: 17.7 us -> 32.4 us
  local copies, waits for them, and re-layouts: 15.5 us -> 1.34 us
  starting transfers between devices: 5.71 us -> 18.8 us
    all_to_all x1 -> x0, blocking collectives: 18.2 us -> none  [local(): lax.all_to_all(send, 'seq', split_axis=0, concat_axis=0, tiled=True, axis...]
    unnamed x41 -> x4, local copies, waits for them, and re-layouts: 15.5 us -> 1.34 us
    all_to_all x0 -> x1, starting transfers between devices: none -> 11.2 us  [local(): lax.all_to_all(send, 'seq', split_axis=0, concat_axis=0, tiled=True, axis...]
    pallas_call x1 -> x2, Pallas kernels: 4.79 us -> 13.4 us  [the longest x1 7.16 us: local(): pl.pallas_call(functools.partial(prepare_kernel, heads), grid=(blocks,),...]
    pallas_call x1, Pallas kernels: 5.49 us -> 8.01 us  [local(): pl.pallas_call(functools.partial(diagonal_kernel, heads), grid=(blocks,),...]
    pallas_call x1, Pallas kernels: 3.35 us -> 5.28 us  [local(): pl.pallas_call(functools.partial(norm_kernel, heads, sources, float(total...]
    all_to_all x1, starting transfers between devices: 5.71 us -> 7.57 us  [local(): lax.all_to_all(back, 'seq', split_axis=0, concat_axis=0, tiled=True, axis...]
    pallas_call x1, Pallas kernels: 2.9 us -> 4.58 us  [local(): pl.pallas_call(functools.partial(state_kernel, heads, blocks), out_shape=...]
  transfers between devices with their start and end apart: 1 -> 2, of which waited for: 0 -> 0; matrix products, arithmetic and copies ran while one was open for 1% -> 0% of each run, Pallas kernels for 5% -> 14%
where the time goes in v2:
time: 113 us; the launch traced here: 111 us
  blocking collectives  57.7 us (51%)
  Pallas kernels  32.4 us (29%)
  starting transfers between devices  18.8 us (17%)
  local copies, waits for them, and re-layouts  1.34 us (1%)
    all_to_all x1, blocking collectives, local(): lax.all_to_all(gated, 'head', split_axis=0, concat_axis=0, tiled=True)  57.7 us
    all_to_all x1, starting transfers between devices, local(): lax.all_to_all(send, 'seq', split_axis=0, concat_axis=0, tiled=True, axis...  11.2 us
    pallas_call x1, Pallas kernels, local(): pl.pallas_call(functools.partial(diagonal_kernel, heads), grid=(blocks,),...  8.01 us
    all_to_all x1, starting transfers between devices, local(): lax.all_to_all(back, 'seq', split_axis=0, concat_axis=0, tiled=True, axis...  7.57 us
    pallas_call x1, Pallas kernels, local(): pl.pallas_call(functools.partial(prepare_kernel, heads), grid=(blocks,),...  7.16 us
    pallas_call x1, Pallas kernels, local(): pl.pallas_call(gate_kernel, grid=(blocks,), out_shape=jax.ShapeDtypeStruc...  6.19 us
    pallas_call x1, Pallas kernels, local(): pl.pallas_call(functools.partial(norm_kernel, heads, sources, float(total...  5.28 us
    pallas_call x1, Pallas kernels, local(): pl.pallas_call(functools.partial(state_kernel, heads, blocks), out_shape=...  4.58 us
  transfers between devices with their start and end apart: 2, of which 0 were waited for; matrix products, arithmetic and copies ran while one was open for 0% of the time, Pallas kernels for 14%

profile of v2, /device:TPU:7, one launch (start us, length us, event | category | flops | bytes accessed | tf_op | source)
XLA Modules:
  0.0 110.9 jit_solution(6812077770131449860)
XLA Ops:
  0.6 4.6 %shard_map.122 = (f32[48,256]{1,0:T(8,128)}, f32[48,256]{1,0:T(8,128)}, bf16[6,128,640]{2,1,0:T(8,128)(2,1)}, f32[48,128]{1,0:T(8,128)}, bf16[128,768]{1,0:T(8,128)(2,1)}) custom-call(f32[5]{0:T(128)} %dt_bias.1, f32[5]{0:T(128)} %a_rate.1, s32[6]{0:T(128)} %traj.1, f32[5,1536]{1,0:T(8,128)} %dt_raw.1, bf16[320,1536]{1,0:T(8,128)(2,1)} %bitcast.11, ...), custom_call_target="tpu_custom_call" | custom-call | flops 300000000 | bytes 4000000 | tf_op jit(solution)/shard_map/pallas_call | solution.py:299
  5.2 11.2 %all-to-all-start = ((bf16[16,8,768]{2,1,0:T(8,128)(2,1)}), bf16[16,8,768]{2,1,0:T(8,128)(2,1)S(1)}, u32[]{:S(2)}, u32[]{:S(2)}) async-start(bf16[16,8,768]{2,1,0:T(8,128)(2,1)} %bitcast.17), calls=%async_computation | async-start | bytes 393216 | tf_op jit(solution)/shard_map/all_to_all | solution.py:356
  16.5 8.0 %shard_map.123 = (f32[1536,640]{1,0:T(8,128)}, f32[1536,128]{1,0:T(8,128)}, f32[8,128]{1,0:T(8,128)}) custom-call(f32[5]{0:T(128)} %d_skip.1, bf16[320,1536]{1,0:T(8,128)(2,1)} %bitcast.12, bf16[320,1536]{1,0:T(8,128)(2,1)} %bitcast.14, bf16[1536,128]{1,0:T(8,128)(2,1)} %bmat.1, bf16[1536,128]{1,0:T(8,128)(2,1)} %cmat.3, ...), custom_call_target="tpu_custom_call" | custom-call | flops 2000000000 | bytes 16000000 | tf_op jit(solution)/shard_map/pallas_call | solution.py:330
  24.5 0.0 all-to-all-done
  24.5 0.0 copy-start
  24.5 0.7 copy-done
  25.2 1.2 %shard_map.124._ = bf16[128,640]{1,0:T(8,128)(2,1)} custom-call(bf16[128,768]{1,0:T(8,128)(2,1)S(1)} %bitcast.9, f32[8,128]{1,0:T(8,128)S(1)} %copy-done), custom_call_target="tpu_custom_call" | custom-call | tf_op jit(solution)/shard_map/pallas_call | solution.py:359
  26.3 7.6 %all-to-all-start.1 = ((bf16[16,8,640]{2,1,0:T(8,128)(2,1)}), bf16[16,8,640]{2,1,0:T(8,128)(2,1)S(1)}, u32[]{:S(2)}, u32[]{:S(2)}) async-start(bf16[16,8,640]{2,1,0:T(8,128)(2,1)} %bitcast.5), calls=%async_computation.1 | async-start | bytes 327680 | tf_op jit(solution)/shard_map/all_to_all | solution.py:366
  33.9 7.2 %shard_map.125 = (f32[1536,640]{1,0:T(8,128)}, bf16[1536,640]{1,0:T(8,128)(2,1)}) custom-call(bf16[320,1536]{1,0:T(8,128)(2,1)} %bitcast.15, f32[1536,640]{1,0:T(8,128)} %get-tuple-element.16.y_local, f32[1536,128]{1,0:T(8,128)} %get-tuple-element.17.reach, bf16[128,640]{1,0:T(8,128)(2,1)} %shard_map.124._), custom_call_target="tpu_custom_call" | custom-call | flops 300000000 | bytes 16000000 | tf_op jit(solution)/shard_map/pallas_call | solution.py:369
  41.1 0.0 all-to-all-done.1
  41.1 0.0 copy-start.1
  41.1 0.7 copy-done.1
  41.7 6.2 %shard_map.126 = bf16[1536,640]{1,0:T(8,128)(2,1)} custom-call(f32[1536,640]{1,0:T(8,128)} %get-tuple-element.20.base, bf16[1536,640]{1,0:T(8,128)(2,1)} %get-tuple-element.21.slope, bf16[1536,128]{1,0:T(8,128)(2,1)} %cmat.3, bf16[128,640]{1,0:T(8,128)(2,1)} %bitcast.16), custom_call_target="tpu_custom_call" | custom-call | flops 260000000 | bytes 8000000 | tf_op jit(solution)/shard_map/pallas_call | solution.py:389
  47.9 57.7 %all_to_all.31.gathered = bf16[16,96,640]{2,1,0:T(8,128)(2,1)} all-to-all(bf16[16,96,640]{2,1,0:T(8,128)(2,1)} %bitcast.10), channel_id=1, replica_groups=mesh['seq'=32,'head'=16] {'head'}, dimensions={0} | all-to-all | bytes 3932160 | tf_op jit(solution)/shard_map/all_to_all | solution.py:406
  105.7 5.3 %shard_map.127 = (bf16[96,5120]{1,0:T(8,128)(2,1)}, bf16[96,5120]{1,0:T(8,128)(2,1)}) custom-call(bf16[16,96,640]{2,1,0:T(8,128)(2,1)} %all_to_all.31.gathered, f32[1,5120]{1,0:T(1,128)} %bitcast.18), custom_call_target="tpu_custom_call" | custom-call | tf_op jit(solution)/shard_map/pallas_call | solution.py:410
Async XLA Ops:
  5.2 19.3 %all-to-all-start = ((bf16[16,8,768]{2,1,0:T(8,128)(2,1)}), bf16[16,8,768]{2,1,0:T(8,128)(2,1)S(1)}, u32[]{:S(2)}, u32[]{:S(2)}) async-start(bf16[16,8,768]{2,1,0:T(8,128)(2,1)} %bitcast.17), calls=%async_computation | async-start | bytes 393216 | tf_op jit(solution)/shard_map/all_to_all | solution.py:356
  24.5 0.7 copy-start
  26.3 14.7 %all-to-all-start.1 = ((bf16[16,8,640]{2,1,0:T(8,128)(2,1)}), bf16[16,8,640]{2,1,0:T(8,128)(2,1)S(1)}, u32[]{:S(2)}, u32[]{:S(2)}) async-start(bf16[16,8,640]{2,1,0:T(8,128)(2,1)} %bitcast.5), calls=%async_computation.1 | async-start | bytes 327680 | tf_op jit(solution)/shard_map/all_to_all | solution.py:366
  41.1 0.7 copy-start.1

commit v3 on v2

v3 whole, which is shorter than its diff:
```python
import functools

import jax
import jax.numpy as jnp
from jax import lax
from jax.experimental import pallas as pl
from jax.experimental.pallas import tpu as pltpu
from jax.sharding import PartitionSpec as P

Q = 256
HALF = 128
LANES = 128
PACK = 8
LOG2E = 1.4426950408889634
MIB = 1024 * 1024
F32 = jnp.float32
BF16 = jnp.bfloat16


def column_of(values):
    place = lax.broadcasted_iota(jnp.int32, (PACK, 1), 0)
    column = jnp.zeros((PACK, 1), F32)
    for h, value in enumerate(values):
        column = jnp.where(place == h, value, column)
    return column


def by_head(per_head, rows):
    low = lax.broadcasted_iota(jnp.int32, (rows, LANES), 1) < LANES // 2
    first = jnp.where(low, per_head[0], per_head[1])
    second = jnp.where(low, per_head[2], per_head[3])
    last = jnp.broadcast_to(per_head[4], (rows, LANES))
    return [first, first, second, second, last]


def feature_rows(main, tan, heads, width):
    order = []
    for pair in range(0, heads, 2):
        for array in (main, tan):
            for h in range(pair, min(pair + 2, heads)):
                order.append((h, array[h * width : (h + 1) * width, :]))
    return order


def split_bf16(x, parts):
    pieces = []
    for _ in range(parts):
        piece = x.astype(BF16)
        pieces.append(piece)
        x = x - piece.astype(F32)
    return pieces


def across(left, right):
    return lax.dot_general(left, right, (((1,), (1,)), ((), ())), preferred_element_type=F32)


def state_kernel(
    heads,
    blocks,
    dt_bias,
    a_rate,
    traj,
    dt_raw,
    xs_hbm,
    dxs_hbm,
    bmat_hbm,
    shifted_out,
    logs_out,
    local_out,
    fin,
    send,
    xs,
    dxs,
    bmat,
    local_in,
    sems,
    out_sems,
):
    width = xs.shape[0] // heads
    chunks = [slice(h * width, min(h + 2, heads) * width) for h in range(0, heads, 2)]
    b_copy = pltpu.make_async_copy(bmat_hbm, bmat, sems.at[2, 0])
    copies = []
    for i, at in enumerate(chunks):
        copies.append(
            [
                pltpu.make_async_copy(xs_hbm.at[at, :], xs.at[at, :], sems.at[0, i]),
                pltpu.make_async_copy(dxs_hbm.at[at, :], dxs.at[at, :], sems.at[1, i]),
            ]
        )
    copies[0][0].start()
    copies[0][1].start()
    b_copy.start()
    for pair_copies in copies[1:]:
        for copy in pair_copies:
            copy.start()
    bias = column_of([dt_bias[h] for h in range(heads)])
    rate = column_of([a_rate[h] * LOG2E for h in range(heads)])
    raw = jnp.concatenate([dt_raw[...], jnp.zeros((PACK - heads, blocks * Q), F32)], axis=0)
    pre = jnp.concatenate([raw[:, c * Q : (c + 1) * Q] for c in range(blocks)], axis=0)
    pre = pre + jnp.concatenate([bias] * blocks, axis=0)
    step = jnp.maximum(pre, 0.0) + jnp.log1p(jnp.exp(-jnp.abs(pre)))
    upper = (
        lax.broadcasted_iota(jnp.int32, (Q, Q), 0) <= lax.broadcasted_iota(jnp.int32, (Q, Q), 1)
    ).astype(BF16)
    logs = jnp.zeros((blocks * PACK, Q), F32)
    for piece in split_bf16(-(step * jnp.concatenate([rate] * blocks, axis=0)), 3)[::-1]:
        logs = logs + jnp.dot(piece, upper, preferred_element_type=F32)
    shifted = logs - jnp.log2(step)
    shifted_out[...] = shifted
    logs_out[...] = logs
    ends = logs[:, Q - 1 : Q]
    weight_in = jnp.exp2(ends - shifted)
    end_decay = jnp.exp2(ends)

    factor = jnp.ones((PACK, 1), F32)
    keeps = [None]
    for c in range(blocks):
        if c > 0:
            keeps.append(jnp.where(traj[c] == traj[c - 1], 1.0, 0.0))
            factor = factor * keeps[c]
        fin[c * PACK : (c + 1) * PACK, :] = jnp.broadcast_to(factor, (PACK, LANES))
        factor = factor * end_decay[c * PACK : (c + 1) * PACK, :]
    copies_out = []
    b_copy.wait()
    for i, at in enumerate(chunks):
        for copy in copies[i]:
            copy.wait()
        members = [h for h in range(2 * i, min(2 * i + 2, heads))] * 2
        place = slice(2 * at.start, 2 * at.stop)
        state = jnp.zeros((len(members) * width, LANES), F32)
        for c in range(blocks):
            here = slice(c * Q, (c + 1) * Q)
            if c > 0:
                state = state * keeps[c]
            local_in[c, place, :] = state.astype(BF16)
            both = jnp.concatenate([xs[at, here], dxs[at, here]], axis=0).astype(F32)
            scale = jnp.concatenate(
                [
                    jnp.broadcast_to(
                        weight_in[c * PACK + h : c * PACK + h + 1, :], (width, Q)
                    )
                    for h in members
                ],
                axis=0,
            )
            gained = jnp.dot(
                (both * scale).astype(BF16), bmat[here, :], preferred_element_type=F32
            )
            decay = jnp.concatenate(
                [
                    jnp.broadcast_to(
                        end_decay[c * PACK + h : c * PACK + h + 1, :], (width, LANES)
                    )
                    for h in members
                ],
                axis=0,
            )
            state = state * decay + gained
        rows = pl.ds(place.start, place.stop - place.start)
        leaving = pltpu.make_async_copy(
            local_in.at[:, rows, :], local_out.at[:, rows, :], out_sems.at[i]
        )
        leaving.start()
        copies_out.append(leaving)
        send[:, place] = state.T.astype(BF16)
    lane = lax.broadcasted_iota(jnp.int32, (1, LANES), 1)
    notes = jnp.zeros((1, LANES), F32)
    for h in range(heads):
        rest = factor[h : h + 1, :]
        for k in range(3):
            piece = rest.astype(BF16).astype(F32)
            notes = jnp.where(lane == k * heads + h, piece, notes)
            rest = rest - piece
    notes = jnp.where(lane == 3 * heads, traj[0].astype(F32), notes)
    notes = jnp.where(lane == 3 * heads + 1, traj[blocks - 1].astype(F32), notes)
    send[:, heads * LANES :] = jnp.broadcast_to(notes, (LANES, LANES)).astype(BF16)
    for leaving in copies_out:
        leaving.wait()


def scan_kernel(heads, count, got, _, back, hold):
    width = heads * LANES
    everything = got[...].astype(F32)
    carried = jnp.zeros((PACK, width), F32)
    last_id = None
    for s in range(count):
        at = slice(s * PACK, (s + 1) * PACK)
        notes = everything[at, width:]
        factor = []
        for h in range(heads):
            total = notes[:, h : h + 1]
            for k in range(1, 3):
                total = total + notes[:, k * heads + h : k * heads + h + 1]
            factor.append(total)
        first_id = notes[:, 3 * heads : 3 * heads + 1]
        if s > 0:
            carried = jnp.where(first_id == last_id, carried, 0.0)
        hold[at, :] = carried
        last_id = notes[:, 3 * heads + 1 : 3 * heads + 2]
        carried = jnp.concatenate(by_head(factor, PACK), axis=1) * carried + everything[at, :width]
    back[...] = hold[...].astype(BF16)


def diagonal_kernel(
    heads, d_skip, xs, dxs, zgate, bmat, cmat, shifted, logs, local_in, fin, base, slope
):
    width = xs.shape[0] // heads
    block = pl.program_id(0)
    mine = pl.ds(pl.multiple_of(block * PACK, PACK), PACK)
    log_rows, shifted_rows = logs[mine, :], shifted[mine, :]
    decays = jnp.exp2(log_rows)
    table = jnp.concatenate(
        [log_rows, decays, decays * fin[mine, 0:1], jnp.zeros((LANES - 3 * PACK, Q), F32)], axis=0
    ).T
    scores = across(cmat[...], bmat[...])
    causal = lax.broadcasted_iota(jnp.int32, (HALF, HALF), 0) >= lax.broadcasted_iota(
        jnp.int32, (HALF, HALF), 1
    )
    unit = (
        lax.broadcasted_iota(jnp.int32, (Q, Q), 0) == lax.broadcasted_iota(jnp.int32, (Q, Q), 1)
    ).astype(BF16)
    nothing = jnp.zeros((HALF, HALF), BF16)
    z = across(unit, zgate[...])
    gate = z / (1.0 + jnp.exp(-z))
    gate_last = gate[:, 2 * LANES :]
    gates = [
        gate[:, :LANES],
        gate[:, LANES : 2 * LANES],
        jnp.concatenate([gate_last, gate_last], axis=1),
    ]
    low = lax.broadcasted_iota(jnp.int32, (Q, LANES), 1) < LANES // 2

    def weights(h):
        log_t = table[:, h : h + 1]
        log_s = shifted_rows[h : h + 1, :]
        near = scores[:HALF, :HALF] * jnp.exp2(log_t[:HALF] - log_s[:, :HALF])
        far = scores[HALF:, :HALF] * jnp.exp2(log_t[HALF:] - log_s[:, :HALF])
        last = scores[HALF:, HALF:] * jnp.exp2(log_t[HALF:] - log_s[:, HALF:])
        top = jnp.concatenate([jnp.where(causal, near, 0.0).astype(BF16), nothing], axis=1)
        bottom = jnp.concatenate([far, jnp.where(causal, last, 0.0)], axis=1).astype(BF16)
        return [top, bottom]

    carried = across(cmat[...], local_in[0])
    decay = by_head([table[:, PACK + h : PACK + h + 1] for h in range(heads)], Q)
    reach = by_head([table[:, 2 * PACK + h : 2 * PACK + h + 1] for h in range(heads)], Q)
    skip = by_head([d_skip[h] for h in range(heads)], 1)
    rows = feature_rows(xs[...], dxs[...], heads, width)
    for pair in range(0, heads, 2):
        members = range(pair, min(pair + 2, heads))
        operand = jnp.concatenate([part for h, part in rows if h in members], axis=0)
        left = [piece for h in members for piece in weights(h)] + [unit]
        sums = across(jnp.concatenate(left, axis=0), operand)
        count = len(members)
        for i in range(count):
            tile = pair + i
            at = slice(tile * LANES, (tile + 1) * LANES)
            lanes = slice(i * LANES, (i + 1) * LANES)
            diagonal = sums[:Q, lanes]
            if count == 2:
                diagonal = jnp.where(low, diagonal, sums[Q : 2 * Q, lanes])
            plain = sums[count * Q :, lanes]
            y = diagonal + carried[:, at] * decay[tile] + plain * skip[tile]
            base[:, at] = (y * gates[pair // 2]).astype(BF16)
        at = slice(pair // 2 * LANES, (pair // 2 + 1) * LANES)
        slope[:, at] = (reach[pair] * gates[pair // 2]).astype(BF16)


def gate_kernel(blocks, heads, base, slope, cmat_hbm, incoming, out, cmat, sems):
    copies = []
    for c in range(blocks):
        here = pl.ds(c * Q, Q)
        copies.append(
            pltpu.make_async_copy(cmat_hbm.at[here, :], cmat.at[here, :], sems.at[c])
        )
    for copy in copies:
        copy.start()
    state = incoming[...]
    for c in range(blocks):
        here = slice(c * Q, (c + 1) * Q)
        copies[c].wait()
        carried = jnp.dot(cmat[here, :], state, preferred_element_type=F32)
        for i in range(heads):
            at = slice(i * LANES, (i + 1) * LANES)
            gain = slope[here, i // 2 * LANES : (i // 2 + 1) * LANES].astype(F32)
            out[here, at] = (base[here, at].astype(F32) + carried[:, at] * gain).astype(BF16)


def norm_kernel(
    heads, sources, strip, strips, total_width, gathered, gain, normed, normed_tan, held, sems
):
    half = LANES // 2
    width = heads * half
    copies = []
    for r in range(strips):
        here = slice(r * strip, (r + 1) * strip)
        main_parts, tan_parts = [], []
        for s in range(sources):
            tiles = [
                gathered[s, here, i * LANES : (i + 1) * LANES].astype(F32) for i in range(heads)
            ]
            main_parts += [tiles[0], tiles[2], tiles[4][:, :half]]
            tan_parts += [tiles[1], tiles[3], tiles[4][:, half:]]
        mains, tans = [], []
        for s in range(0, sources, 2):
            mains.append(jnp.concatenate(main_parts[3 * s : 3 * s + 6], axis=1))
            tans.append(jnp.concatenate(tan_parts[3 * s : 3 * s + 6], axis=1))
        square = sum(m * m for m in mains)
        cross = sum(m * t for m, t in zip(mains, tans))
        mean_square = jnp.sum(square, axis=1, keepdims=True) / total_width
        mean_cross = jnp.sum(cross, axis=1, keepdims=True) / total_width
        inv_rms = lax.rsqrt(mean_square + 1e-05)
        pull = inv_rms * inv_rms * inv_rms * mean_cross
        for i, (m, t) in enumerate(zip(mains, tans)):
            at = slice(i * 2 * width, (i + 1) * 2 * width)
            g = gain[:, at]
            held[0, here, at] = (g * m * inv_rms).astype(BF16)
            held[1, here, at] = (g * (t * inv_rms - m * pull)).astype(BF16)
        for k, target in enumerate((normed, normed_tan)):
            copy = pltpu.make_async_copy(held.at[k, here, :], target.at[here, :], sems.at[k, r])
            copy.start()
            copies.append(copy)
    for copy in copies:
        copy.wait()


def whole(shape):
    return pl.BlockSpec(shape, lambda *_: (0,) * len(shape))


SMEM_SPEC = pl.BlockSpec(memory_space=pltpu.SMEM)


def local(xs, dxs, zgate, bmat, cmat, dt_raw, dt_bias, a_rate, d_skip, gain, traj_ids):
    tokens, inner = xs.shape
    heads = dt_raw.shape[0]
    blocks = tokens // Q
    wide = heads * LANES
    state_rows = bmat.shape[1]
    sources = lax.axis_size("head")
    seq_size = lax.axis_size("seq")
    group = state_rows // PACK
    groups = [list(range(g, g + group)) for g in range(0, seq_size, group)]
    params = pltpu.CompilerParams(vmem_limit_bytes=60 * MIB)
    roomy = pltpu.CompilerParams(vmem_limit_bytes=32 * MIB)
    small = pltpu.CompilerParams(vmem_limit_bytes=16 * MIB)
    in_vmem = pl.BlockSpec(memory_space=pltpu.VMEM)
    in_hbm = pl.BlockSpec(memory_space=pl.ANY)
    xs, dxs, zgate, bmat, cmat = [
        pltpu.with_memory_space_constraint(array, pltpu.HBM)
        for array in (xs.T, dxs.T, zgate.T, bmat, cmat)
    ]

    def pinned(array):
        return pltpu.with_memory_space_constraint(array, pltpu.VMEM)

    shifted, logs, local_in, fin, send = pl.pallas_call(
        functools.partial(state_kernel, heads, blocks),
        out_shape=(
            pltpu.VMEM((blocks * PACK, Q), F32),
            pltpu.VMEM((blocks * PACK, Q), F32),
            jax.ShapeDtypeStruct((blocks, wide, state_rows), BF16),
            pltpu.VMEM((blocks * PACK, LANES), F32),
            pltpu.VMEM((state_rows, wide + LANES), BF16),
        ),
        in_specs=[SMEM_SPEC] * 3 + [in_vmem] + [in_hbm] * 3,
        out_specs=(in_vmem, in_vmem, in_hbm, in_vmem, in_vmem),
        scratch_shapes=[
            pltpu.VMEM((inner, tokens), BF16),
            pltpu.VMEM((inner, tokens), BF16),
            pltpu.VMEM((tokens, state_rows), BF16),
            pltpu.VMEM((blocks, wide, state_rows), BF16),
            pltpu.SemaphoreType.DMA((3, len(range(0, heads, 2)))),
            pltpu.SemaphoreType.DMA((len(range(0, heads, 2)),)),
        ],
        compiler_params=params,
        cost_estimate=pl.CostEstimate(
            flops=300_000_000, bytes_accessed=4_000_000, transcendentals=30_000
        ),
    )(dt_bias, a_rate, traj_ids, dt_raw, xs, dxs, bmat)

    def token_block(width):
        return pl.BlockSpec((Q, width), lambda c: (c, 0))

    def feature_block(width):
        return pl.BlockSpec((width, Q), lambda c: (0, c))

    lean = (heads + 1) // 2 * LANES
    base, slope = pl.pallas_call(
        functools.partial(diagonal_kernel, heads),
        grid=(blocks,),
        out_shape=(
            pltpu.VMEM((tokens, wide), BF16),
            pltpu.VMEM((tokens, lean), BF16),
        ),
        in_specs=[
            SMEM_SPEC,
            feature_block(inner),
            feature_block(inner),
            feature_block(inner),
            token_block(state_rows),
            token_block(state_rows),
            in_vmem,
            in_vmem,
            pl.BlockSpec((1, wide, state_rows), lambda c: (c, 0, 0)),
            in_vmem,
        ],
        out_specs=(token_block(wide), token_block(lean)),
        compiler_params=roomy,
        cost_estimate=pl.CostEstimate(
            flops=2_000_000_000, bytes_accessed=16_000_000, transcendentals=2_000_000
        ),
    )(
        d_skip,
        xs,
        dxs,
        zgate,
        bmat,
        cmat,
        pinned(shifted),
        pinned(logs),
        pltpu.with_memory_space_constraint(local_in, pltpu.HBM),
        pinned(fin),
    )

    got = lax.all_to_all(
        send, "seq", split_axis=0, concat_axis=0, tiled=True, axis_index_groups=groups
    )
    back = pl.pallas_call(
        functools.partial(scan_kernel, heads, group),
        out_shape=jax.ShapeDtypeStruct((state_rows, wide), BF16),
        in_specs=[in_vmem, in_hbm],
        scratch_shapes=[pltpu.VMEM((state_rows, wide), F32)],
        compiler_params=small,
    )(got, pinned(slope))
    incoming = lax.all_to_all(
        back, "seq", split_axis=0, concat_axis=0, tiled=True, axis_index_groups=groups
    )
    gated = pl.pallas_call(
        functools.partial(gate_kernel, blocks, heads),
        out_shape=jax.ShapeDtypeStruct((tokens, wide), BF16),
        in_specs=[in_vmem, in_vmem, in_hbm, in_vmem],
        scratch_shapes=[
            pltpu.VMEM((tokens, state_rows), BF16),
            pltpu.SemaphoreType.DMA((blocks,)),
        ],
        compiler_params=small,
        cost_estimate=pl.CostEstimate(
            flops=260_000_000, bytes_accessed=6_000_000, transcendentals=0
        ),
    )(
        pinned(base),
        pinned(slope),
        cmat,
        incoming,
    )

    gathered = lax.all_to_all(gated, "head", split_axis=0, concat_axis=0, tiled=True)
    mine = tokens // sources
    strip = 16
    strips = mine // strip
    total = inner * sources
    return pl.pallas_call(
        functools.partial(norm_kernel, heads, sources, strip, strips, float(total)),
        out_shape=(
            jax.ShapeDtypeStruct((mine, total), BF16),
            jax.ShapeDtypeStruct((mine, total), BF16),
        ),
        in_specs=[in_vmem] * 2,
        out_specs=(in_hbm, in_hbm),
        scratch_shapes=[
            pltpu.VMEM((2, mine, total), BF16),
            pltpu.SemaphoreType.DMA((2, strips)),
        ],
        compiler_params=small,
    )(gathered.reshape(sources, mine, wide), gain.reshape(1, total))


def solution(mesh):
    placed = (
        P("seq", "head"),
        P("seq", "head"),
        P("seq", "head"),
        P("seq", None),
        P("seq", None),
        P("head", "seq"),
        P("head"),
        P("head"),
        P("head"),
        P(),
        P("seq"),
    )
    return jax.shard_map(
        local,
        mesh=mesh,
        in_specs=placed,
        out_specs=(P(("seq", "head"), None), P(("seq", "head"), None)),
        check_vma=False,
    )
```

time: 113 us -> 104 us (0.920)
  blocking collectives: 57.7 us -> 72 us
  Pallas kernels: 32.4 us -> 18.2 us
  starting transfers between devices: 18.8 us -> 11.2 us
  local copies, waits for them, and re-layouts: 1.34 us -> 0.01 us
    all_to_all x0 -> x1, blocking collectives: none -> 14.3 us  [local(): lax.all_to_all(back, 'seq', split_axis=0, concat_axis=0, tiled=True, axis...]
    pallas_call x3 -> x2, Pallas kernels: 18.6 us -> 4.75 us  [the longest x1 2.39 us: local(): pl.pallas_call(functools.partial(gate_kernel, blocks, heads), out_shape=j...]
    all_to_all x1 -> x0, starting transfers between devices: 7.57 us -> none  [local(): lax.all_to_all(back, 'seq', split_axis=0, concat_axis=0, tiled=True, axis...]
    unnamed x4, local copies, waits for them, and re-layouts: 1.34 us -> 0.01 us
  transfers between devices with their start and end apart: 2 -> 1, of which waited for: 0 -> 0; matrix products, arithmetic and copies ran while one was open for 0% -> 0% of each run, Pallas kernels for 14% -> 8%
where the time goes in v3:
time: 104 us; the launch traced here: 102 us
  blocking collectives  72 us (69%)
  Pallas kernels  18.2 us (18%)
  starting transfers between devices  11.2 us (11%)
    all_to_all x1, blocking collectives, local(): lax.all_to_all(gated, 'head', split_axis=0, concat_axis=0, tiled=True)  57.7 us
    all_to_all x1, blocking collectives, local(): lax.all_to_all(back, 'seq', split_axis=0, concat_axis=0, tiled=True, axis...  14.3 us
    all_to_all x1, starting transfers between devices, local(): lax.all_to_all(send, 'seq', split_axis=0, concat_axis=0, tiled=True, axis...  11.2 us
    pallas_call x1, Pallas kernels, local(): pl.pallas_call(functools.partial(diagonal_kernel, heads), grid=(blocks,),...  8.11 us
    pallas_call x1, Pallas kernels, local(): pl.pallas_call(functools.partial(state_kernel, heads, blocks), out_shape=...  4.81 us
    pallas_call x1, Pallas kernels, local(): pl.pallas_call(functools.partial(gate_kernel, blocks, heads), out_shape=j...  2.39 us
    pallas_call x1, Pallas kernels, local(): pl.pallas_call(functools.partial(norm_kernel, heads, sources, strip, stri...  2.36 us
  transfers between devices with their start and end apart: 1, of which 0 were waited for; matrix products, arithmetic and copies ran while one was open for 0% of the time, Pallas kernels for 8%

profile of v3, /device:TPU:7, one launch (start us, length us, event | category | flops | bytes accessed | tf_op | source)
XLA Modules:
  0.0 102.1 jit_solution(13938030663374979938)
XLA Ops:
  0.6 0.0 copy-start.1
  0.6 4.8 %shard_map.122 = (f32[48,256]{1,0:T(8,128)S(1)}, f32[48,256]{1,0:T(8,128)S(1)}, bf16[6,640,128]{2,1,0:T(8,128)(2,1)}, f32[48,128]{1,0:T(8,128)S(1)}, bf16[128,768]{1,0:T(8,128)(2,1)}) custom-call(f32[5]{0:T(128)} %dt_bias.1, f32[5]{0:T(128)} %a_rate.1, s32[6]{0:T(128)} %traj.1, f32[5,1536]{1,0:T(8,128)} %dt_raw.1, bf16[320,1536]{1,0:T(8,128)(2,1)} %bitcast.14, ...), custom_call_target="tpu_custom_call" | custom-call | flops 300000000 | bytes 4000000 | tf_op jit(solution)/shard_map/pallas_call | solution.py:357
  5.5 11.2 %all-to-all-start = ((bf16[16,8,768]{2,1,0:T(8,128)(2,1)}), bf16[16,8,768]{2,1,0:T(8,128)(2,1)S(1)}, u32[]{:S(2)}, u32[]{:S(2)}) async-start(bf16[16,8,768]{2,1,0:T(8,128)(2,1)} %bitcast.3), calls=%async_computation | async-start | bytes 393216 | tf_op jit(solution)/shard_map/all_to_all | solution.py:426
  16.7 0.0 copy-done.1
  16.7 8.1 %shard_map.123 = (bf16[1536,640]{1,0:T(8,128)(2,1)S(1)}, bf16[1536,384]{1,0:T(8,128)(2,1)S(1)}) custom-call(f32[5]{0:T(128)S(1)} %copy-done.1, bf16[320,1536]{1,0:T(8,128)(2,1)} %bitcast.15, bf16[320,1536]{1,0:T(8,128)(2,1)} %bitcast.17, bf16[320,1536]{1,0:T(8,128)(2,1)} %bitcast.18, bf16[1536,128]{1,0:T(8,128)(2,1)} %bmat.1, bf16[1536,128]{1,0:T(8,128)(2,1)} %cmat_hbm.1, ...), custom_call_target="tpu_custom_call" | custom-call | flops 2000000000 | bytes 16000000 | tf_op jit(solution)/shard_map/pallas_call | solution.py:389
  24.8 0.0 all-to-all-done
  24.8 0.5 shard_map.124
  25.3 14.3 %all_to_all.31 = bf16[16,8,640]{2,1,0:T(8,128)(2,1)S(1)} all-to-all(bf16[16,8,640]{2,1,0:T(8,128)(2,1)S(1)} %bitcast.12), channel_id=1, replica_groups={{0,16,32,48,64,80,96,112,128,144,160,176,192,208,224,240},{256,272,288,..., dimensions={0} | all-to-all | bytes 327680 | tf_op jit(solution)/shard_map/all_to_all | solution.py:436
  39.6 2.4 %shard_map.125 = bf16[1536,640]{1,0:T(8,128)(2,1)S(1)} custom-call(bf16[1536,640]{1,0:T(8,128)(2,1)S(1)} %get-tuple-element.13.base, bf16[1536,384]{1,0:T(8,128)(2,1)S(1)} %get-tuple-element.14._.slope, bf16[1536,128]{1,0:T(8,128)(2,1)} %cmat_hbm.1, bf16[128,640]{1,0:T(8,128)(2,1)S(1)} %bitcast.11), custom_call_target="tpu_custom_call" | custom-call | flops 260000000 | bytes 6000000 | tf_op jit(solution)/shard_map/pallas_call | solution.py:439
  42.0 0.0 copy-start
  42.0 57.7 %all_to_all.32.gathered = bf16[16,96,640]{2,1,0:T(8,128)(2,1)S(1)} all-to-all(bf16[16,96,640]{2,1,0:T(8,128)(2,1)S(1)} %bitcast.9), channel_id=1, replica_groups=mesh['seq'=32,'head'=16] {'head'}, dimensions={0} | all-to-all | bytes 3932160 | tf_op jit(solution)/shard_map/all_to_all | solution.py:458
  99.7 0.0 copy-done
  99.7 2.4 %shard_map.126 = (bf16[96,5120]{1,0:T(8,128)(2,1)}, bf16[96,5120]{1,0:T(8,128)(2,1)}) custom-call(bf16[16,96,640]{2,1,0:T(8,128)(2,1)S(1)} %all_to_all.32.gathered, f32[1,5120]{1,0:T(1,128)S(1)} %bitcast.13), custom_call_target="tpu_custom_call" | custom-call | tf_op jit(solution)/shard_map/pallas_call | solution.py:463
Async XLA Ops:
  0.6 16.1 %copy-start.1 = (f32[5]{0:T(128)S(1)}, f32[5]{0:T(128)}, u32[]{:S(2)}) copy-start(f32[5]{0:T(128)} %d_skip.1) | copy-start | bytes 64
  5.5 19.4 %all-to-all-start = ((bf16[16,8,768]{2,1,0:T(8,128)(2,1)}), bf16[16,8,768]{2,1,0:T(8,128)(2,1)S(1)}, u32[]{:S(2)}, u32[]{:S(2)}) async-start(bf16[16,8,768]{2,1,0:T(8,128)(2,1)} %bitcast.3), calls=%async_computation | async-start | bytes 393216 | tf_op jit(solution)/shard_map/all_to_all | solution.py:426
  42.0 57.7 %copy-start = (f32[5120]{0:T(1024)S(1)}, f32[5120]{0:T(1024)}, u32[]{:S(2)}) copy-start(f32[5120]{0:T(1024)} %param.20) | copy-start | bytes 61444

commit v4 on v3

--- a/solution.py
+++ b/solution.py
@@ -61,7 +61,7 @@
     dt_bias,
     a_rate,
     traj,
-    dt_raw,
+    dt_hbm,
     xs_hbm,
     dxs_hbm,
     bmat_hbm,
@@ -74,12 +74,15 @@
     dxs,
     bmat,
     local_in,
+    dt_raw,
     sems,
     out_sems,
 ):
     width = xs.shape[0] // heads
     chunks = [slice(h * width, min(h + 2, heads) * width) for h in range(0, heads, 2)]
     b_copy = pltpu.make_async_copy(bmat_hbm, bmat, sems.at[2, 0])
+    dt_copy = pltpu.make_async_copy(dt_hbm, dt_raw, sems.at[2, 1])
+    dt_copy.start()
     copies = []
     for i, at in enumerate(chunks):
         copies.append(
@@ -96,6 +99,7 @@
             copy.start()
     bias = column_of([dt_bias[h] for h in range(heads)])
     rate = column_of([a_rate[h] * LOG2E for h in range(heads)])
+    dt_copy.wait()
     raw = jnp.concatenate([dt_raw[...], jnp.zeros((PACK - heads, blocks * Q), F32)], axis=0)
     pre = jnp.concatenate([raw[:, c * Q : (c + 1) * Q] for c in range(blocks)], axis=0)
     pre = pre + jnp.concatenate([bias] * blocks, axis=0)
@@ -209,10 +213,10 @@
     block = pl.program_id(0)
     mine = pl.ds(pl.multiple_of(block * PACK, PACK), PACK)
     log_rows, shifted_rows = logs[mine, :], shifted[mine, :]
-    decays = jnp.exp2(log_rows)
-    table = jnp.concatenate(
-        [log_rows, decays, decays * fin[mine, 0:1], jnp.zeros((LANES - 3 * PACK, Q), F32)], axis=0
-    ).T
+    table = jnp.concatenate([log_rows, jnp.zeros((LANES - PACK, Q), F32)], axis=0).T
+    log_wide = [jnp.broadcast_to(table[:, h : h + 1], (Q, LANES)) for h in range(heads)]
+    decays = [jnp.exp2(wide) for wide in log_wide]
+    through = fin[mine, 0:1]
     scores = across(cmat[...], bmat[...])
     causal = lax.broadcasted_iota(jnp.int32, (HALF, HALF), 0) >= lax.broadcasted_iota(
         jnp.int32, (HALF, HALF), 1
@@ -222,7 +226,7 @@
     ).astype(BF16)
     nothing = jnp.zeros((HALF, HALF), BF16)
     z = across(unit, zgate[...])
-    gate = z / (1.0 + jnp.exp(-z))
+    gate = z * (0.5 + 0.5 * jnp.tanh(0.5 * z))
     gate_last = gate[:, 2 * LANES :]
     gates = [
         gate[:, :LANES],
@@ -232,7 +236,7 @@
     low = lax.broadcasted_iota(jnp.int32, (Q, LANES), 1) < LANES // 2
 
     def weights(h):
-        log_t = table[:, h : h + 1]
+        log_t = log_wide[h]
         log_s = shifted_rows[h : h + 1, :]
         near = scores[:HALF, :HALF] * jnp.exp2(log_t[:HALF] - log_s[:, :HALF])
         far = scores[HALF:, :HALF] * jnp.exp2(log_t[HALF:] - log_s[:, :HALF])
@@ -242,8 +246,7 @@
         return [top, bottom]
 
     carried = across(cmat[...], local_in[0])
-    decay = by_head([table[:, PACK + h : PACK + h + 1] for h in range(heads)], Q)
-    reach = by_head([table[:, 2 * PACK + h : 2 * PACK + h + 1] for h in range(heads)], Q)
+    factors = [through[h : h + 1, :] for h in range(heads)]
     skip = by_head([d_skip[h] for h in range(heads)], 1)
     rows = feature_rows(xs[...], dxs[...], heads, width)
     for pair in range(0, heads, 2):
@@ -252,6 +255,10 @@
         left = [piece for h in members for piece in weights(h)] + [unit]
         sums = across(jnp.concatenate(left, axis=0), operand)
         count = len(members)
+        decay, factor = decays[pair], factors[pair]
+        if count == 2:
+            decay = jnp.where(low, decay, decays[pair + 1])
+            factor = jnp.where(low, factor, factors[pair + 1])
         for i in range(count):
             tile = pair + i
             at = slice(tile * LANES, (tile + 1) * LANES)
@@ -260,25 +267,16 @@
             if count == 2:
                 diagonal = jnp.where(low, diagonal, sums[Q : 2 * Q, lanes])
             plain = sums[count * Q :, lanes]
-            y = diagonal + carried[:, at] * decay[tile] + plain * skip[tile]
+            y = diagonal + carried[:, at] * decay + plain * skip[tile]
             base[:, at] = (y * gates[pair // 2]).astype(BF16)
         at = slice(pair // 2 * LANES, (pair // 2 + 1) * LANES)
-        slope[:, at] = (reach[pair] * gates[pair // 2]).astype(BF16)
-
-
-def gate_kernel(blocks, heads, base, slope, cmat_hbm, incoming, out, cmat, sems):
-    copies = []
-    for c in range(blocks):
-        here = pl.ds(c * Q, Q)
-        copies.append(
-            pltpu.make_async_copy(cmat_hbm.at[here, :], cmat.at[here, :], sems.at[c])
-        )
-    for copy in copies:
-        copy.start()
+        slope[:, at] = (decay * factor * gates[pair // 2]).astype(BF16)
+
+
+def gate_kernel(blocks, heads, base, slope, cmat, incoming, out):
     state = incoming[...]
     for c in range(blocks):
         here = slice(c * Q, (c + 1) * Q)
-        copies[c].wait()
         carried = jnp.dot(cmat[here, :], state, preferred_element_type=F32)
         for i in range(heads):
             at = slice(i * LANES, (i + 1) * LANES)
@@ -346,9 +344,10 @@
     small = pltpu.CompilerParams(vmem_limit_bytes=16 * MIB)
     in_vmem = pl.BlockSpec(memory_space=pltpu.VMEM)
     in_hbm = pl.BlockSpec(memory_space=pl.ANY)
-    xs, dxs, zgate, bmat, cmat = [
+    c_plain = cmat
+    xs, dxs, zgate, bmat, cmat, dt_raw = [
         pltpu.with_memory_space_constraint(array, pltpu.HBM)
-        for array in (xs.T, dxs.T, zgate.T, bmat, cmat)
+        for array in (xs.T, dxs.T, zgate.T, bmat, cmat, dt_raw)
     ]
 
     def pinned(array):
@@ -363,13 +362,14 @@
             pltpu.VMEM((blocks * PACK, LANES), F32),
             pltpu.VMEM((state_rows, wide + LANES), BF16),
         ),
-        in_specs=[SMEM_SPEC] * 3 + [in_vmem] + [in_hbm] * 3,
+        in_specs=[SMEM_SPEC] * 3 + [in_hbm] * 4,
         out_specs=(in_vmem, in_vmem, in_hbm, in_vmem, in_vmem),
         scratch_shapes=[
             pltpu.VMEM((inner, tokens), BF16),
             pltpu.VMEM((inner, tokens), BF16),
             pltpu.VMEM((tokens, state_rows), BF16),
             pltpu.VMEM((blocks, wide, state_rows), BF16),
+            pltpu.VMEM((heads, tokens), F32),
             pltpu.SemaphoreType.DMA((3, len(range(0, heads, 2)))),
             pltpu.SemaphoreType.DMA((len(range(0, heads, 2)),)),
         ],
@@ -439,11 +439,7 @@
     gated = pl.pallas_call(
         functools.partial(gate_kernel, blocks, heads),
         out_shape=jax.ShapeDtypeStruct((tokens, wide), BF16),
-        in_specs=[in_vmem, in_vmem, in_hbm, in_vmem],
-        scratch_shapes=[
-            pltpu.VMEM((tokens, state_rows), BF16),
-            pltpu.SemaphoreType.DMA((blocks,)),
-        ],
+        in_specs=[in_vmem] * 4,
         compiler_params=small,
         cost_estimate=pl.CostEstimate(
             flops=260_000_000, bytes_accessed=6_000_000, transcendentals=0
@@ -451,7 +447,7 @@
     )(
         pinned(base),
         pinned(slope),
-        cmat,
+        pinned(c_plain),
         incoming,
     )
 

time: 104 us -> 101 us (0.971)
  Pallas kernels: 18.2 us -> 15.5 us
    pallas_call x1, Pallas kernels: 2.39 us -> 0.77 us  [local(): pl.pallas_call(functools.partial(gate_kernel, blocks, heads), out_shape=j...]
    pallas_call x1, Pallas kernels: 8.11 us -> 7.04 us  [local(): pl.pallas_call(functools.partial(diagonal_kernel, heads), grid=(blocks,),...]
  transfers between devices with their start and end apart: 1 -> 1, of which waited for: 0 -> 0; matrix products, arithmetic and copies ran while one was open for 0% -> 0% of each run, Pallas kernels for 8% -> 7%
where the time goes in v4:
time: 101 us; the launch traced here: 99.4 us
  blocking collectives  71.9 us (71%)
  Pallas kernels  15.5 us (15%)
  starting transfers between devices  11.2 us (11%)
    all_to_all x1, blocking collectives, local(): lax.all_to_all(gated, 'head', split_axis=0, concat_axis=0, tiled=True)  57.7 us
    all_to_all x1, blocking collectives, local(): lax.all_to_all(back, 'seq', split_axis=0, concat_axis=0, tiled=True, axis...  14.3 us
    all_to_all x1, starting transfers between devices, local(): lax.all_to_all(send, 'seq', split_axis=0, concat_axis=0, tiled=True, axis...  11.2 us
    pallas_call x1, Pallas kernels, local(): pl.pallas_call(functools.partial(diagonal_kernel, heads), grid=(blocks,),...  7.04 us
    pallas_call x1, Pallas kernels, local(): pl.pallas_call(functools.partial(state_kernel, heads, blocks), out_shape=...  4.79 us
    pallas_call x1, Pallas kernels, local(): pl.pallas_call(functools.partial(norm_kernel, heads, sources, strip, stri...  2.36 us
  transfers between devices with their start and end apart: 1, of which 0 were waited for; matrix products, arithmetic and copies ran while one was open for 0% of the time, Pallas kernels for 7%

profile of v4, /device:TPU:7, one launch (start us, length us, event | category | flops | bytes accessed | tf_op | source)
XLA Modules:
  0.0 99.4 jit_solution(14440579703502736872)
XLA Ops:
  0.6 0.0 copy-start.2
  0.6 4.8 %shard_map.122 = (f32[48,256]{1,0:T(8,128)S(1)}, f32[48,256]{1,0:T(8,128)S(1)}, bf16[6,640,128]{2,1,0:T(8,128)(2,1)}, f32[48,128]{1,0:T(8,128)S(1)}, bf16[128,768]{1,0:T(8,128)(2,1)}) custom-call(f32[5]{0:T(128)} %dt_bias.1, f32[5]{0:T(128)} %a_rate.1, s32[6]{0:T(128)} %traj.1, f32[5,1536]{1,0:T(8,128)} %dt_hbm.1, bf16[320,1536]{1,0:T(8,128)(2,1)} %bitcast.14, ...), custom_call_target="tpu_custom_call" | custom-call | flops 300000000 | bytes 4000000 | tf_op jit(solution)/shard_map/pallas_call | solution.py:356
  5.4 11.2 %all-to-all-start = ((bf16[16,8,768]{2,1,0:T(8,128)(2,1)}), bf16[16,8,768]{2,1,0:T(8,128)(2,1)S(1)}, u32[]{:S(2)}, u32[]{:S(2)}) async-start(bf16[16,8,768]{2,1,0:T(8,128)(2,1)} %bitcast.3), calls=%async_computation | async-start | bytes 393216 | tf_op jit(solution)/shard_map/all_to_all | solution.py:426
  16.7 0.0 copy-done.2
  16.7 7.0 %shard_map.123 = (bf16[1536,640]{1,0:T(8,128)(2,1)S(1)}, bf16[1536,384]{1,0:T(8,128)(2,1)S(1)}) custom-call(f32[5]{0:T(128)S(1)} %copy-done.2, bf16[320,1536]{1,0:T(8,128)(2,1)} %bitcast.15, bf16[320,1536]{1,0:T(8,128)(2,1)} %bitcast.17, bf16[320,1536]{1,0:T(8,128)(2,1)} %bitcast.18, bf16[1536,128]{1,0:T(8,128)(2,1)} %bmat.1, bf16[1536,128]{1,0:T(8,128)(2,1)} %cmat.3, ...), custom_call_target="tpu_custom_call" | custom-call | flops 2000000000 | bytes 16000000 | tf_op jit(solution)/shard_map/pallas_call | solution.py:389
  23.7 0.0 all-to-all-done
  23.8 0.0 copy-start
  23.8 0.5 shard_map.124
  24.3 14.3 %all_to_all.31 = bf16[16,8,640]{2,1,0:T(8,128)(2,1)S(1)} all-to-all(bf16[16,8,640]{2,1,0:T(8,128)(2,1)S(1)} %bitcast.12), channel_id=1, replica_groups={{0,16,32,48,64,80,96,112,128,144,160,176,192,208,224,240},{256,272,288,..., dimensions={0} | all-to-all | bytes 327680 | tf_op jit(solution)/shard_map/all_to_all | solution.py:436
  38.5 0.0 copy-done
  38.5 0.8 shard_map.125
  39.3 0.0 copy-start.1
  39.3 57.7 %all_to_all.32.gathered = bf16[16,96,640]{2,1,0:T(8,128)(2,1)S(1)} all-to-all(bf16[16,96,640]{2,1,0:T(8,128)(2,1)S(1)} %bitcast.9), channel_id=1, replica_groups=mesh['seq'=32,'head'=16] {'head'}, dimensions={0} | all-to-all | bytes 3932160 | tf_op jit(solution)/shard_map/all_to_all | solution.py:454
  97.0 0.0 copy-done.1
  97.0 2.4 %shard_map.126 = (bf16[96,5120]{1,0:T(8,128)(2,1)}, bf16[96,5120]{1,0:T(8,128)(2,1)}) custom-call(bf16[16,96,640]{2,1,0:T(8,128)(2,1)S(1)} %all_to_all.32.gathered, f32[1,5120]{1,0:T(1,128)S(1)} %bitcast.13), custom_call_target="tpu_custom_call" | custom-call | tf_op jit(solution)/shard_map/pallas_call | solution.py:459
Async XLA Ops:
  0.6 16.1 %copy-start.2 = (f32[5]{0:T(128)S(1)}, f32[5]{0:T(128)}, u32[]{:S(2)}) copy-start(f32[5]{0:T(128)} %d_skip.1) | copy-start | bytes 64
  5.4 18.3 %all-to-all-start = ((bf16[16,8,768]{2,1,0:T(8,128)(2,1)}), bf16[16,8,768]{2,1,0:T(8,128)(2,1)S(1)}, u32[]{:S(2)}, u32[]{:S(2)}) async-start(bf16[16,8,768]{2,1,0:T(8,128)(2,1)} %bitcast.3), calls=%async_computation | async-start | bytes 393216 | tf_op jit(solution)/shard_map/all_to_all | solution.py:426
  23.8 14.8 %copy-start = (bf16[1536,128]{1,0:T(8,128)(2,1)S(1)}, bf16[1536,128]{1,0:T(8,128)(2,1)}, u32[]{:S(2)}) copy-start(bf16[1536,128]{1,0:T(8,128)(2,1)} %cmat.3) | copy-start | bytes 1179652
  39.3 57.7 %copy-start.1 = (f32[5120]{0:T(1024)S(1)}, f32[5120]{0:T(1024)}, u32[]{:S(2)}) copy-start(f32[5120]{0:T(1024)} %param.20) | copy-start | bytes 61444

commit v5 on v4

--- a/solution.py
+++ b/solution.py
@@ -11,7 +11,6 @@
 HALF = 128
 LANES = 128
 PACK = 8
-LOG2E = 1.4426950408889634
 MIB = 1024 * 1024
 F32 = jnp.float32
 BF16 = jnp.bfloat16
@@ -58,9 +57,9 @@
 def state_kernel(
     heads,
     blocks,
-    dt_bias,
-    a_rate,
-    traj,
+    bias_hbm,
+    rate_hbm,
+    traj_hbm,
     dt_hbm,
     xs_hbm,
     dxs_hbm,
@@ -75,8 +74,12 @@
     bmat,
     local_in,
     dt_raw,
+    dt_bias,
+    a_rate,
+    traj,
     sems,
     out_sems,
+    small_sems,
 ):
     width = xs.shape[0] // heads
     chunks = [slice(h * width, min(h + 2, heads) * width) for h in range(0, heads, 2)]
@@ -94,11 +97,21 @@
     copies[0][0].start()
     copies[0][1].start()
     b_copy.start()
+    small_copies = [
+        pltpu.make_async_copy(source, target, small_sems.at[i])
+        for i, (source, target) in enumerate(
+            ((bias_hbm, dt_bias), (rate_hbm, a_rate), (traj_hbm, traj))
+        )
+    ]
+    for copy in small_copies:
+        copy.start()
     for pair_copies in copies[1:]:
         for copy in pair_copies:
             copy.start()
+    for copy in small_copies:
+        copy.wait()
     bias = column_of([dt_bias[h] for h in range(heads)])
-    rate = column_of([a_rate[h] * LOG2E for h in range(heads)])
+    rate = column_of([a_rate[h] for h in range(heads)])
     dt_copy.wait()
     raw = jnp.concatenate([dt_raw[...], jnp.zeros((PACK - heads, blocks * Q), F32)], axis=0)
     pre = jnp.concatenate([raw[:, c * Q : (c + 1) * Q] for c in range(blocks)], axis=0)
@@ -110,12 +123,12 @@
     logs = jnp.zeros((blocks * PACK, Q), F32)
     for piece in split_bf16(-(step * jnp.concatenate([rate] * blocks, axis=0)), 3)[::-1]:
         logs = logs + jnp.dot(piece, upper, preferred_element_type=F32)
-    shifted = logs - jnp.log2(step)
+    shifted = logs - jnp.log(step)
     shifted_out[...] = shifted
     logs_out[...] = logs
     ends = logs[:, Q - 1 : Q]
-    weight_in = jnp.exp2(ends - shifted)
-    end_decay = jnp.exp2(ends)
+    weight_in = jnp.exp(ends - shifted)
+    end_decay = jnp.exp(ends)
 
     factor = jnp.ones((PACK, 1), F32)
     keeps = [None]
@@ -215,7 +228,7 @@
     log_rows, shifted_rows = logs[mine, :], shifted[mine, :]
     table = jnp.concatenate([log_rows, jnp.zeros((LANES - PACK, Q), F32)], axis=0).T
     log_wide = [jnp.broadcast_to(table[:, h : h + 1], (Q, LANES)) for h in range(heads)]
-    decays = [jnp.exp2(wide) for wide in log_wide]
+    decays = [jnp.exp(wide) for wide in log_wide]
     through = fin[mine, 0:1]
     scores = across(cmat[...], bmat[...])
     causal = lax.broadcasted_iota(jnp.int32, (HALF, HALF), 0) >= lax.broadcasted_iota(
@@ -238,9 +251,9 @@
     def weights(h):
         log_t = log_wide[h]
         log_s = shifted_rows[h : h + 1, :]
-        near = scores[:HALF, :HALF] * jnp.exp2(log_t[:HALF] - log_s[:, :HALF])
-        far = scores[HALF:, :HALF] * jnp.exp2(log_t[HALF:] - log_s[:, :HALF])
-        last = scores[HALF:, HALF:] * jnp.exp2(log_t[HALF:] - log_s[:, HALF:])
+        near = scores[:HALF, :HALF] * jnp.exp(log_t[:HALF] - log_s[:, :HALF])
+        far = scores[HALF:, :HALF] * jnp.exp(log_t[HALF:] - log_s[:, :HALF])
+        last = scores[HALF:, HALF:] * jnp.exp(log_t[HALF:] - log_s[:, HALF:])
         top = jnp.concatenate([jnp.where(causal, near, 0.0).astype(BF16), nothing], axis=1)
         bottom = jnp.concatenate([far, jnp.where(causal, last, 0.0)], axis=1).astype(BF16)
         return [top, bottom]
@@ -362,7 +375,7 @@
             pltpu.VMEM((blocks * PACK, LANES), F32),
             pltpu.VMEM((state_rows, wide + LANES), BF16),
         ),
-        in_specs=[SMEM_SPEC] * 3 + [in_hbm] * 4,
+        in_specs=[in_hbm] * 7,
         out_specs=(in_vmem, in_vmem, in_hbm, in_vmem, in_vmem),
         scratch_shapes=[
             pltpu.VMEM((inner, tokens), BF16),
@@ -370,8 +383,12 @@
             pltpu.VMEM((tokens, state_rows), BF16),
             pltpu.VMEM((blocks, wide, state_rows), BF16),
             pltpu.VMEM((heads, tokens), F32),
+            pltpu.SMEM((heads,), F32),
+            pltpu.SMEM((heads,), F32),
+            pltpu.SMEM((blocks,), jnp.int32),
             pltpu.SemaphoreType.DMA((3, len(range(0, heads, 2)))),
             pltpu.SemaphoreType.DMA((len(range(0, heads, 2)),)),
+            pltpu.SemaphoreType.DMA((3,)),
         ],
         compiler_params=params,
         cost_estimate=pl.CostEstimate(

time: 101 us -> 100 us (0.990)
  no operation moved by 1% of the time
where the time goes in v5:
time: 100 us; the launch traced here: 98.7 us
  blocking collectives  72 us (72%)
  Pallas kernels  14.8 us (15%)
  starting transfers between devices  11.2 us (11%)
    all_to_all x1, blocking collectives, local(): lax.all_to_all(gated, 'head', split_axis=0, concat_axis=0, tiled=True)  57.7 us
    all_to_all x1, blocking collectives, local(): lax.all_to_all(back, 'seq', split_axis=0, concat_axis=0, tiled=True, axis...  14.3 us
    all_to_all x1, starting transfers between devices, local(): lax.all_to_all(send, 'seq', split_axis=0, concat_axis=0, tiled=True, axis...  11.2 us
    pallas_call x1, Pallas kernels, local(): pl.pallas_call(functools.partial(diagonal_kernel, heads), grid=(blocks,),...  7.16 us
    pallas_call x1, Pallas kernels, local(): pl.pallas_call(functools.partial(state_kernel, heads, blocks), out_shape=...  4.01 us
    pallas_call x1, Pallas kernels, local(): pl.pallas_call(functools.partial(norm_kernel, heads, sources, strip, stri...  2.36 us
  transfers between devices with their start and end apart: 1, of which 0 were waited for; matrix products, arithmetic and copies ran while one was open for 0% of the time, Pallas kernels for 7%

profile of v5, /device:TPU:7, one launch (start us, length us, event | category | flops | bytes accessed | tf_op | source)
XLA Modules:
  0.0 98.7 jit_solution(2609705305653347531)
XLA Ops:
  0.6 0.0 copy-start.2
  0.6 4.0 %shard_map.122 = (f32[48,256]{1,0:T(8,128)S(1)}, f32[48,256]{1,0:T(8,128)S(1)}, bf16[6,640,128]{2,1,0:T(8,128)(2,1)}, f32[48,128]{1,0:T(8,128)S(1)}, bf16[128,768]{1,0:T(8,128)(2,1)}) custom-call(f32[5]{0:T(128)} %bias_hbm.1, f32[5]{0:T(128)} %rate_hbm.1, s32[6]{0:T(128)} %traj_hbm.1, f32[5,1536]{1,0:T(8,128)} %dt_hbm.1, bf16[320,1536]{1,0:T(8,128)(2,1)} %bitcast.14, ...), custom_call_target="tpu_custom_call" | custom-call | flops 300000000 | bytes 4000000 | tf_op jit(solution)/shard_map/pallas_call | solution.py:369
  4.7 11.2 %all-to-all-start = ((bf16[16,8,768]{2,1,0:T(8,128)(2,1)}), bf16[16,8,768]{2,1,0:T(8,128)(2,1)S(1)}, u32[]{:S(2)}, u32[]{:S(2)}) async-start(bf16[16,8,768]{2,1,0:T(8,128)(2,1)} %bitcast.3), calls=%async_computation | async-start | bytes 393216 | tf_op jit(solution)/shard_map/all_to_all | solution.py:443
  15.9 0.0 copy-done.2
  15.9 7.2 %shard_map.123 = (bf16[1536,640]{1,0:T(8,128)(2,1)S(1)}, bf16[1536,384]{1,0:T(8,128)(2,1)S(1)}) custom-call(f32[5]{0:T(128)S(1)} %copy-done.2, bf16[320,1536]{1,0:T(8,128)(2,1)} %bitcast.15, bf16[320,1536]{1,0:T(8,128)(2,1)} %bitcast.17, bf16[320,1536]{1,0:T(8,128)(2,1)} %bitcast.18, bf16[1536,128]{1,0:T(8,128)(2,1)} %bmat.1, bf16[1536,128]{1,0:T(8,128)(2,1)} %cmat.3, ...), custom_call_target="tpu_custom_call" | custom-call | flops 2000000000 | bytes 16000000 | tf_op jit(solution)/shard_map/pallas_call | solution.py:406
  23.1 0.0 all-to-all-done
  23.1 0.0 copy-start
  23.1 0.5 shard_map.124
  23.6 14.3 %all_to_all.31 = bf16[16,8,640]{2,1,0:T(8,128)(2,1)S(1)} all-to-all(bf16[16,8,640]{2,1,0:T(8,128)(2,1)S(1)} %bitcast.12), channel_id=1, replica_groups={{0,16,32,48,64,80,96,112,128,144,160,176,192,208,224,240},{256,272,288,..., dimensions={0} | all-to-all | bytes 327680 | tf_op jit(solution)/shard_map/all_to_all | solution.py:453
  37.9 0.0 copy-done
  37.9 0.8 shard_map.125
  38.6 0.0 copy-start.1
  38.7 57.7 %all_to_all.32.gathered = bf16[16,96,640]{2,1,0:T(8,128)(2,1)S(1)} all-to-all(bf16[16,96,640]{2,1,0:T(8,128)(2,1)S(1)} %bitcast.9), channel_id=1, replica_groups=mesh['seq'=32,'head'=16] {'head'}, dimensions={0} | all-to-all | bytes 3932160 | tf_op jit(solution)/shard_map/all_to_all | solution.py:471
  96.3 0.0 copy-done.1
  96.3 2.4 %shard_map.126 = (bf16[96,5120]{1,0:T(8,128)(2,1)}, bf16[96,5120]{1,0:T(8,128)(2,1)}) custom-call(bf16[16,96,640]{2,1,0:T(8,128)(2,1)S(1)} %all_to_all.32.gathered, f32[1,5120]{1,0:T(1,128)S(1)} %bitcast.13), custom_call_target="tpu_custom_call" | custom-call | tf_op jit(solution)/shard_map/pallas_call | solution.py:476
Async XLA Ops:
  0.6 15.3 %copy-start.2 = (f32[5]{0:T(128)S(1)}, f32[5]{0:T(128)}, u32[]{:S(2)}) copy-start(f32[5]{0:T(128)} %d_skip.1) | copy-start | bytes 64
  4.7 18.4 %all-to-all-start = ((bf16[16,8,768]{2,1,0:T(8,128)(2,1)}), bf16[16,8,768]{2,1,0:T(8,128)(2,1)S(1)}, u32[]{:S(2)}, u32[]{:S(2)}) async-start(bf16[16,8,768]{2,1,0:T(8,128)(2,1)} %bitcast.3), calls=%async_computation | async-start | bytes 393216 | tf_op jit(solution)/shard_map/all_to_all | solution.py:443
  23.1 14.8 %copy-start = (bf16[1536,128]{1,0:T(8,128)(2,1)S(1)}, bf16[1536,128]{1,0:T(8,128)(2,1)}, u32[]{:S(2)}) copy-start(bf16[1536,128]{1,0:T(8,128)(2,1)} %cmat.3) | copy-start | bytes 1179652
  38.6 57.7 %copy-start.1 = (f32[5120]{0:T(1024)S(1)}, f32[5120]{0:T(1024)}, u32[]{:S(2)}) copy-start(f32[5120]{0:T(1024)} %param.20) | copy-start | bytes 61444

commit v6 on v5

--- a/solution.py
+++ b/solution.py
@@ -86,17 +86,17 @@
     b_copy = pltpu.make_async_copy(bmat_hbm, bmat, sems.at[2, 0])
     dt_copy = pltpu.make_async_copy(dt_hbm, dt_raw, sems.at[2, 1])
     dt_copy.start()
-    copies = []
-    for i, at in enumerate(chunks):
-        copies.append(
-            [
-                pltpu.make_async_copy(xs_hbm.at[at, :], xs.at[at, :], sems.at[0, i]),
-                pltpu.make_async_copy(dxs_hbm.at[at, :], dxs.at[at, :], sems.at[1, i]),
-            ]
-        )
-    copies[0][0].start()
-    copies[0][1].start()
-    b_copy.start()
+    head_rows = chunks[0].stop
+    parts = [pl.ds(0, head_rows), pl.ds(head_rows, xs.shape[0] - head_rows)]
+    copies = [
+        [
+            pltpu.make_async_copy(xs_hbm.at[part, :], xs.at[part, :], sems.at[0, i]),
+            pltpu.make_async_copy(dxs_hbm.at[part, :], dxs.at[part, :], sems.at[1, i]),
+        ]
+        for i, part in enumerate(parts)
+    ] + [[] for _ in chunks[2:]]
+    for copy in copies[0] + [b_copy] + copies[1]:
+        copy.start()
     small_copies = [
         pltpu.make_async_copy(source, target, small_sems.at[i])
         for i, (source, target) in enumerate(
@@ -105,9 +105,6 @@
     ]
     for copy in small_copies:
         copy.start()
-    for pair_copies in copies[1:]:
-        for copy in pair_copies:
-            copy.start()
     for copy in small_copies:
         copy.wait()
     bias = column_of([dt_bias[h] for h in range(heads)])

time: 100 us -> 100 us (level)
  no operation moved by 1% of the time
where the time goes in v6:
time: 100 us; the launch traced here: 98.5 us
  blocking collectives  72 us (72%)
  Pallas kernels  14.6 us (15%)
  starting transfers between devices  11.2 us (11%)
    all_to_all x1, blocking collectives, local(): lax.all_to_all(gated, 'head', split_axis=0, concat_axis=0, tiled=True)  57.7 us
    all_to_all x1, blocking collectives, local(): lax.all_to_all(back, 'seq', split_axis=0, concat_axis=0, tiled=True, axis...  14.3 us
    all_to_all x1, starting transfers between devices, local(): lax.all_to_all(send, 'seq', split_axis=0, concat_axis=0, tiled=True, axis...  11.2 us
    pallas_call x1, Pallas kernels, local(): pl.pallas_call(functools.partial(diagonal_kernel, heads), grid=(blocks,),...  7.16 us
    pallas_call x1, Pallas kernels, local(): pl.pallas_call(functools.partial(state_kernel, heads, blocks), out_shape=...  3.81 us
    pallas_call x1, Pallas kernels, local(): pl.pallas_call(functools.partial(norm_kernel, heads, sources, strip, stri...  2.36 us
  transfers between devices with their start and end apart: 1, of which 0 were waited for; matrix products, arithmetic and copies ran while one was open for 0% of the time, Pallas kernels for 7%

profile of v6, /device:TPU:7, one launch (start us, length us, event | category | flops | bytes accessed | tf_op | source)
XLA Modules:
  0.0 98.5 jit_solution(3080854767826291591)
XLA Ops:
  0.6 0.0 copy-start.2
  0.6 3.8 %shard_map.122 = (f32[48,256]{1,0:T(8,128)S(1)}, f32[48,256]{1,0:T(8,128)S(1)}, bf16[6,640,128]{2,1,0:T(8,128)(2,1)}, f32[48,128]{1,0:T(8,128)S(1)}, bf16[128,768]{1,0:T(8,128)(2,1)}) custom-call(f32[5]{0:T(128)} %bias_hbm.1, f32[5]{0:T(128)} %rate_hbm.1, s32[6]{0:T(128)} %traj_hbm.1, f32[5,1536]{1,0:T(8,128)} %dt_hbm.1, bf16[320,1536]{1,0:T(8,128)(2,1)} %bitcast.14, ...), custom_call_target="tpu_custom_call" | custom-call | flops 300000000 | bytes 4000000 | tf_op jit(solution)/shard_map/pallas_call | solution.py:366
  4.5 11.2 %all-to-all-start = ((bf16[16,8,768]{2,1,0:T(8,128)(2,1)}), bf16[16,8,768]{2,1,0:T(8,128)(2,1)S(1)}, u32[]{:S(2)}, u32[]{:S(2)}) async-start(bf16[16,8,768]{2,1,0:T(8,128)(2,1)} %bitcast.3), calls=%async_computation | async-start | bytes 393216 | tf_op jit(solution)/shard_map/all_to_all | solution.py:440
  15.7 0.0 copy-done.2
  15.7 7.2 %shard_map.123 = (bf16[1536,640]{1,0:T(8,128)(2,1)S(1)}, bf16[1536,384]{1,0:T(8,128)(2,1)S(1)}) custom-call(f32[5]{0:T(128)S(1)} %copy-done.2, bf16[320,1536]{1,0:T(8,128)(2,1)} %bitcast.15, bf16[320,1536]{1,0:T(8,128)(2,1)} %bitcast.17, bf16[320,1536]{1,0:T(8,128)(2,1)} %bitcast.18, bf16[1536,128]{1,0:T(8,128)(2,1)} %bmat.1, bf16[1536,128]{1,0:T(8,128)(2,1)} %cmat.3, ...), custom_call_target="tpu_custom_call" | custom-call | flops 2000000000 | bytes 16000000 | tf_op jit(solution)/shard_map/pallas_call | solution.py:403
  22.9 0.0 all-to-all-done
  22.9 0.0 copy-start
  22.9 0.5 shard_map.124
  23.4 14.3 %all_to_all.31 = bf16[16,8,640]{2,1,0:T(8,128)(2,1)S(1)} all-to-all(bf16[16,8,640]{2,1,0:T(8,128)(2,1)S(1)} %bitcast.12), channel_id=1, replica_groups={{0,16,32,48,64,80,96,112,128,144,160,176,192,208,224,240},{256,272,288,..., dimensions={0} | all-to-all | bytes 327680 | tf_op jit(solution)/shard_map/all_to_all | solution.py:450
  37.7 0.0 copy-done
  37.7 0.8 shard_map.125
  38.4 0.0 copy-start.1
  38.5 57.7 %all_to_all.32.gathered = bf16[16,96,640]{2,1,0:T(8,128)(2,1)S(1)} all-to-all(bf16[16,96,640]{2,1,0:T(8,128)(2,1)S(1)} %bitcast.9), channel_id=1, replica_groups=mesh['seq'=32,'head'=16] {'head'}, dimensions={0} | all-to-all | bytes 3932160 | tf_op jit(solution)/shard_map/all_to_all | solution.py:468
  96.2 0.0 copy-done.1
  96.2 2.4 %shard_map.126 = (bf16[96,5120]{1,0:T(8,128)(2,1)}, bf16[96,5120]{1,0:T(8,128)(2,1)}) custom-call(bf16[16,96,640]{2,1,0:T(8,128)(2,1)S(1)} %all_to_all.32.gathered, f32[1,5120]{1,0:T(1,128)S(1)} %bitcast.13), custom_call_target="tpu_custom_call" | custom-call | tf_op jit(solution)/shard_map/pallas_call | solution.py:473
Async XLA Ops:
  0.6 15.1 %copy-start.2 = (f32[5]{0:T(128)S(1)}, f32[5]{0:T(128)}, u32[]{:S(2)}) copy-start(f32[5]{0:T(128)} %d_skip.1) | copy-start | bytes 64
  4.5 18.4 %all-to-all-start = ((bf16[16,8,768]{2,1,0:T(8,128)(2,1)}), bf16[16,8,768]{2,1,0:T(8,128)(2,1)S(1)}, u32[]{:S(2)}, u32[]{:S(2)}) async-start(bf16[16,8,768]{2,1,0:T(8,128)(2,1)} %bitcast.3), calls=%async_computation | async-start | bytes 393216 | tf_op jit(solution)/shard_map/all_to_all | solution.py:440
  22.9 14.8 %copy-start = (bf16[1536,128]{1,0:T(8,128)(2,1)S(1)}, bf16[1536,128]{1,0:T(8,128)(2,1)}, u32[]{:S(2)}) copy-start(bf16[1536,128]{1,0:T(8,128)(2,1)} %cmat.3) | copy-start | bytes 1179652
  38.4 57.7 %copy-start.1 = (f32[5120]{0:T(1024)S(1)}, f32[5120]{0:T(1024)}, u32[]{:S(2)}) copy-start(f32[5120]{0:T(1024)} %param.20) | copy-start | bytes 61444

commit v7 on v6

--- a/solution.py
+++ b/solution.py
@@ -231,11 +231,8 @@
     causal = lax.broadcasted_iota(jnp.int32, (HALF, HALF), 0) >= lax.broadcasted_iota(
         jnp.int32, (HALF, HALF), 1
     )
-    unit = (
-        lax.broadcasted_iota(jnp.int32, (Q, Q), 0) == lax.broadcasted_iota(jnp.int32, (Q, Q), 1)
-    ).astype(BF16)
     nothing = jnp.zeros((HALF, HALF), BF16)
-    z = across(unit, zgate[...])
+    z = zgate[...].T.astype(F32)
     gate = z * (0.5 + 0.5 * jnp.tanh(0.5 * z))
     gate_last = gate[:, 2 * LANES :]
     gates = [
@@ -262,8 +259,9 @@
     for pair in range(0, heads, 2):
         members = range(pair, min(pair + 2, heads))
         operand = jnp.concatenate([part for h, part in rows if h in members], axis=0)
-        left = [piece for h in members for piece in weights(h)] + [unit]
+        left = [piece for h in members for piece in weights(h)]
         sums = across(jnp.concatenate(left, axis=0), operand)
+        turned = operand.T.astype(F32)
         count = len(members)
         decay, factor = decays[pair], factors[pair]
         if count == 2:
@@ -276,7 +274,7 @@
             diagonal = sums[:Q, lanes]
             if count == 2:
                 diagonal = jnp.where(low, diagonal, sums[Q : 2 * Q, lanes])
-            plain = sums[count * Q :, lanes]
+            plain = turned[:, lanes]
             y = diagonal + carried[:, at] * decay + plain * skip[tile]
             base[:, at] = (y * gates[pair // 2]).astype(BF16)
         at = slice(pair // 2 * LANES, (pair // 2 + 1) * LANES)
@@ -467,7 +465,7 @@
 
     gathered = lax.all_to_all(gated, "head", split_axis=0, concat_axis=0, tiled=True)
     mine = tokens // sources
-    strip = 16
+    strip = 32
     strips = mine // strip
     total = inner * sources
     return pl.pallas_call(

time: 100 us -> 100 us (level)
  no operation moved by 1% of the time
where the time goes in v7:
time: 100 us; the launch traced here: 98.4 us
  blocking collectives  72 us (72%)
  Pallas kernels  14.5 us (14%)
  starting transfers between devices  11.2 us (11%)
    all_to_all x1, blocking collectives, local(): lax.all_to_all(gated, 'head', split_axis=0, concat_axis=0, tiled=True)  57.7 us
    all_to_all x1, blocking collectives, local(): lax.all_to_all(back, 'seq', split_axis=0, concat_axis=0, tiled=True, axis...  14.3 us
    all_to_all x1, starting transfers between devices, local(): lax.all_to_all(send, 'seq', split_axis=0, concat_axis=0, tiled=True, axis...  11.2 us
    pallas_call x1, Pallas kernels, local(): pl.pallas_call(functools.partial(diagonal_kernel, heads), grid=(blocks,),...  7.09 us
    pallas_call x1, Pallas kernels, local(): pl.pallas_call(functools.partial(state_kernel, heads, blocks), out_shape=...  3.81 us
    pallas_call x1, Pallas kernels, local(): pl.pallas_call(functools.partial(norm_kernel, heads, sources, strip, stri...  2.3 us
  transfers between devices with their start and end apart: 1, of which 0 were waited for; matrix products, arithmetic and copies ran while one was open for 0% of the time, Pallas kernels for 7%

profile of v7, /device:TPU:7, one launch (start us, length us, event | category | flops | bytes accessed | tf_op | source)
XLA Modules:
  0.0 98.4 jit_solution(6374682499914316864)
XLA Ops:
  0.6 0.0 copy-start.2
  0.6 3.8 %shard_map.122 = (f32[48,256]{1,0:T(8,128)S(1)}, f32[48,256]{1,0:T(8,128)S(1)}, bf16[6,640,128]{2,1,0:T(8,128)(2,1)}, f32[48,128]{1,0:T(8,128)S(1)}, bf16[128,768]{1,0:T(8,128)(2,1)}) custom-call(f32[5]{0:T(128)} %bias_hbm.1, f32[5]{0:T(128)} %rate_hbm.1, s32[6]{0:T(128)} %traj_hbm.1, f32[5,1536]{1,0:T(8,128)} %dt_hbm.1, bf16[320,1536]{1,0:T(8,128)(2,1)} %bitcast.14, ...), custom_call_target="tpu_custom_call" | custom-call | flops 300000000 | bytes 4000000 | tf_op jit(solution)/shard_map/pallas_call | solution.py:364
  4.5 11.2 %all-to-all-start = ((bf16[16,8,768]{2,1,0:T(8,128)(2,1)}), bf16[16,8,768]{2,1,0:T(8,128)(2,1)S(1)}, u32[]{:S(2)}, u32[]{:S(2)}) async-start(bf16[16,8,768]{2,1,0:T(8,128)(2,1)} %bitcast.3), calls=%async_computation | async-start | bytes 393216 | tf_op jit(solution)/shard_map/all_to_all | solution.py:438
  15.7 0.0 copy-done.2
  15.7 7.1 %shard_map.123 = (bf16[1536,640]{1,0:T(8,128)(2,1)S(1)}, bf16[1536,384]{1,0:T(8,128)(2,1)S(1)}) custom-call(f32[5]{0:T(128)S(1)} %copy-done.2, bf16[320,1536]{1,0:T(8,128)(2,1)} %bitcast.15, bf16[320,1536]{1,0:T(8,128)(2,1)} %bitcast.17, bf16[320,1536]{1,0:T(8,128)(2,1)} %bitcast.18, bf16[1536,128]{1,0:T(8,128)(2,1)} %bmat.1, bf16[1536,128]{1,0:T(8,128)(2,1)} %cmat.3, ...), custom_call_target="tpu_custom_call" | custom-call | flops 2000000000 | bytes 16000000 | tf_op jit(solution)/shard_map/pallas_call | solution.py:401
  22.8 0.0 all-to-all-done
  22.8 0.0 copy-start
  22.8 0.5 shard_map.124
  23.3 14.3 %all_to_all.31 = bf16[16,8,640]{2,1,0:T(8,128)(2,1)S(1)} all-to-all(bf16[16,8,640]{2,1,0:T(8,128)(2,1)S(1)} %bitcast.12), channel_id=1, replica_groups={{0,16,32,48,64,80,96,112,128,144,160,176,192,208,224,240},{256,272,288,..., dimensions={0} | all-to-all | bytes 327680 | tf_op jit(solution)/shard_map/all_to_all | solution.py:448
  37.6 0.0 copy-done
  37.6 0.8 shard_map.125
  38.4 0.0 copy-start.1
  38.4 57.7 %all_to_all.32.gathered = bf16[16,96,640]{2,1,0:T(8,128)(2,1)S(1)} all-to-all(bf16[16,96,640]{2,1,0:T(8,128)(2,1)S(1)} %bitcast.9), channel_id=1, replica_groups=mesh['seq'=32,'head'=16] {'head'}, dimensions={0} | all-to-all | bytes 3932160 | tf_op jit(solution)/shard_map/all_to_all | solution.py:466
  96.1 0.0 copy-done.1
  96.1 2.3 %shard_map.126 = (bf16[96,5120]{1,0:T(8,128)(2,1)}, bf16[96,5120]{1,0:T(8,128)(2,1)}) custom-call(bf16[16,96,640]{2,1,0:T(8,128)(2,1)S(1)} %all_to_all.32.gathered, f32[1,5120]{1,0:T(1,128)S(1)} %bitcast.13), custom_call_target="tpu_custom_call" | custom-call | tf_op jit(solution)/shard_map/pallas_call | solution.py:471
Async XLA Ops:
  0.6 15.1 %copy-start.2 = (f32[5]{0:T(128)S(1)}, f32[5]{0:T(128)}, u32[]{:S(2)}) copy-start(f32[5]{0:T(128)} %d_skip.1) | copy-start | bytes 64
  4.5 18.4 %all-to-all-start = ((bf16[16,8,768]{2,1,0:T(8,128)(2,1)}), bf16[16,8,768]{2,1,0:T(8,128)(2,1)S(1)}, u32[]{:S(2)}, u32[]{:S(2)}) async-start(bf16[16,8,768]{2,1,0:T(8,128)(2,1)} %bitcast.3), calls=%async_computation | async-start | bytes 393216 | tf_op jit(solution)/shard_map/all_to_all | solution.py:438
  22.8 14.8 %copy-start = (bf16[1536,128]{1,0:T(8,128)(2,1)S(1)}, bf16[1536,128]{1,0:T(8,128)(2,1)}, u32[]{:S(2)}) copy-start(bf16[1536,128]{1,0:T(8,128)(2,1)} %cmat.3) | copy-start | bytes 1179652
  38.4 57.7 %copy-start.1 = (f32[5120]{0:T(1024)S(1)}, f32[5120]{0:T(1024)}, u32[]{:S(2)}) copy-start(f32[5120]{0:T(1024)} %param.20) | copy-start | bytes 61444
